TPU v7x, 32 devices: a whole 2x2x4 slice. The times are simulated.
32 devices in a mesh: ctx: 2 (over y), head: 4 (over x, core), video: 4 (over z).
Axes of the slice: x: 2, y: 2, z: 4, core: 2. Of those that a mesh axis runs over, the one named last changes fastest.
Arguments:
- attention_qkv: bfloat16 [3, 4, 256, 3072], P(None, 'video', 'ctx', 'head'), may hold values from -8 to 8
- inner_qkv: bfloat16 [3, 4, 256, 3072], P(None, 'video', 'ctx', 'head'), may hold values from -3 to 3
- learn_rate: float32 [4, 48, 256], P('video', 'head', 'ctx'), may hold values from 0.001 to 0.01
- segment_id: int32 [4, 256], P('video'), may hold values from 0 to 3, never falling along the last dimension, each value on 1 to 128 neighbouring positions
- video_length: int32 [4], P('video'), may hold values from 128 to 256, as said below
- gate_alpha: float32 [3072], P('head'), may hold values from -1.5 to 1.5
- inner_gain: float32 [48, 64], P('head'), may hold values from 0.5 to 1.5
- inner_shift: float32 [48, 64], P('head'), may hold values from -3 to 3
- first_weight: bfloat16 [48, 64, 256], P('head'), may hold values from -0.75 to 0.75
- first_bias: float32 [48, 256], P('head'), may hold values from -3 to 3
- second_weight: bfloat16 [48, 256, 64], P('head'), may hold values from -0.375 to 0.375
- second_bias: float32 [48, 64], P('head'), may hold values from -3 to 3
- out_weight: bfloat16 [3072, 3072], P('head', 'video'), may hold values from -0.109375 to 0.109375
Outputs:
- mixed: bfloat16 [4, 256, 3072], P('video', 'ctx', 'head')
Inputs may be any that keep to these rules, and one draw needn't show every extreme that they name: `segment_id`: segment numbers never fall along a video; each segment holds 1 to 128 positions and some segment exactly 128. `video_length`: some video is live in all 256 positions.
All inputs are finite; a program needn't handle non-finite values.
Results may differ from a plain program's by a relative error of at most 0.017.
Values may be sent and summed in bfloat16 or wider, within the bound.
A program may use at most 64 MiB of HBM per device.

v0:
```python
from functools import partial

import jax
import jax.numpy as jnp
from jax import lax
from jax.experimental import pallas as pl
from jax.experimental.pallas import tpu as pltpu
from jax.sharding import PartitionSpec as P

HD = 64
MB = 64


gelu_scale = 0.7978845608028654
gelu_cubic = 0.044715


def with_halo(cells, sides, width):
    for axis, dim in sides:
        count = lax.axis_size(axis)
        ends = count - 1
        head = lax.slice_in_dim(cells, 0, width, axis=dim)
        tail = lax.slice_in_dim(cells, cells.shape[dim] - width, cells.shape[dim], axis=dim)
        cells = jnp.concatenate(
            [
                lax.ppermute(tail, axis, [(i, (i + 1) % count) for i in range(ends)]),
                cells,
                lax.ppermute(head, axis, [((i + 1) % count, i) for i in range(ends)]),
            ],
            axis=dim,
        )
    return cells


def matmul_high(first_op, second_op):
    return jnp.matmul(first_op, second_op, precision=lax.Precision.HIGHEST)


def gelu_pair(entries):
    inner_arg = gelu_scale * (entries + gelu_cubic * entries * entries * entries)
    tanh_val = jnp.tanh(inner_arg)
    act_val = 0.5 * entries * (1.0 + tanh_val)
    slope_val = 0.5 * (1.0 + tanh_val) + 0.5 * entries * (
        1.0 - tanh_val * tanh_val
    ) * gelu_scale * (1.0 + 3.0 * gelu_cubic * entries * entries)
    return (act_val, slope_val)


def layer_stats(summed):
    center = summed - jnp.mean(summed, axis=-1, keepdims=True)
    variance = jnp.mean(center * center, axis=-1, keepdims=True)
    inv_std = lax.rsqrt(variance + 1e-06)
    return (center * inv_std, inv_std)


def lower_mask(row_count):
    row_ids = lax.broadcasted_iota(jnp.int32, (row_count, row_count), 0)
    col_ids = lax.broadcasted_iota(jnp.int32, (row_count, row_count), 1)
    return (row_ids >= col_ids).astype(jnp.float32)


def inner_update(inner_state, key_mb, value_mb, rate_mb, norm_gain, norm_shift):
    weight_one, bias_one, weight_two, bias_two = inner_state
    hidden_pre = matmul_high(key_mb, weight_one) + bias_one
    hidden_act, hidden_slope = gelu_pair(hidden_pre)
    output_pre = matmul_high(hidden_act, weight_two) + bias_two
    normed, inv_std = layer_stats(output_pre)
    residual_err = norm_gain * normed + norm_shift - (value_mb - key_mb)
    scaled_err = residual_err * norm_gain
    grad_two = inv_std * (
        scaled_err
        - jnp.mean(scaled_err, axis=-1, keepdims=True)
        - normed * jnp.mean(scaled_err * normed, axis=-1, keepdims=True)
    )
    grad_one = matmul_high(grad_two, weight_two.T) * hidden_slope
    grad_one = grad_one * rate_mb[:, None]
    grad_two = grad_two * rate_mb[:, None]
    new_state = (
        weight_one - matmul_high(key_mb.T, grad_one),
        bias_one - jnp.sum(grad_one, axis=0),
        weight_two - matmul_high(hidden_act.T, grad_two),
        bias_two - jnp.sum(grad_two, axis=0),
    )
    return ((grad_one, hidden_act, grad_two), new_state)


def query_side(inner_state, query_mb, key_mb, grad_pack, norm_gain, norm_shift):
    weight_one, bias_one, weight_two, bias_two = inner_state
    grad_one, hidden_act, grad_two = grad_pack
    causal = lower_mask(query_mb.shape[0])
    first_kernel = (matmul_high(query_mb, key_mb.T) + 1.0) * causal
    query_pre = matmul_high(query_mb, weight_one) + bias_one - matmul_high(first_kernel, grad_one)
    query_act, unused_slope = gelu_pair(query_pre)
    second_kernel = (matmul_high(query_act, hidden_act.T) + 1.0) * causal
    query_out = matmul_high(query_act, weight_two) + bias_two - matmul_high(second_kernel, grad_two)
    normed, unused_inv = layer_stats(query_out)
    return query_mb + norm_gain * normed + norm_shift


def chain_scan(
    keep_queries, inner_state, queries, key_rows, values, rate_vals, norm_gain, norm_shift
):

    def stepper(loop_state, inputs):
        query_mb, key_mb, value_mb, rate_mb = inputs
        grad_pack, new_state = inner_update(
            loop_state, key_mb, value_mb, rate_mb, norm_gain, norm_shift
        )
        return (
            new_state,
            query_side(loop_state, query_mb, key_mb, grad_pack, norm_gain, norm_shift),
        )

    return lax.scan(stepper, inner_state, (queries, key_rows, values, rate_vals))


def pad_heads(array_in, total_heads, fill_value):
    extra = total_heads - array_in.shape[0]
    filler = jnp.full((extra,) + array_in.shape[1:], fill_value, array_in.dtype)
    return jnp.concatenate([array_in, filler], axis=0)


LANE = 128
MESH_ID = pl.DeviceIdType.MESH


def dot_nn(left, right):
    return lax.dot_general(
        left, right, (((1,), (0,)), ((), ())), preferred_element_type=jnp.float32
    )


def dot_nt(left, right):
    return lax.dot_general(
        left, right, (((1,), (1,)), ((), ())), preferred_element_type=jnp.float32
    )


def dot_tn(left, right):
    return lax.dot_general(
        left, right, (((0,), (0,)), ((), ())), preferred_element_type=jnp.float32
    )


def gelu_only(entries):
    inner_arg = gelu_scale * (entries + gelu_cubic * entries * entries * entries)
    return 0.5 * entries * (1.0 + jnp.tanh(inner_arg))


def half_mean(cells, left):
    first = jnp.sum(jnp.where(left, cells, 0.0), axis=-1, keepdims=True)
    second = jnp.sum(jnp.where(left, 0.0, cells), axis=-1, keepdims=True)
    return jnp.where(left, first, second) * (1.0 / HD)


def half_stats(summed, left):
    center = summed - half_mean(summed, left)
    inv_std = lax.rsqrt(half_mean(center * center, left) + 1e-06)
    return (center * inv_std, inv_std)


def split_heads(cells, left):
    wide = cells.astype(jnp.float32)
    return jnp.concatenate(
        [jnp.where(left, wide, 0.0), jnp.where(left, 0.0, wide)], axis=0
    ).astype(cells.dtype)


def fused_kernel(
    aqkv,
    iqkv,
    rate,
    first_w,
    second_w,
    out_w,
    seg,
    length,
    gate,
    gain,
    shift,
    first_b,
    second_b,
    out,
    a_rows,
    i_rows,
    rates,
    fw,
    sw,
    ow,
    w1m,
    w1b,
    w2m,
    w2b,
    b1,
    b2,
    gate_s,
    gain_s,
    shift_s,
    rate_a,
    rate_b,
    bias,
    inner,
    comb,
    gathered,
    parts,
    arrived,
    total,
    landed,
    load_sem,
    y_send,
    y_recv,
    back_send,
    back_recv,
    z_send,
    z_recv,
    own_sem,
    r_send,
    r_recv,
    t_send,
    t_recv,
    low_sem,
    high_sem,
):
    slabs, _, seq, _ = a_rows.shape
    tok = aqkv.shape[2]
    hidden = first_b.shape[1]
    count = lax.axis_size("head")
    c = lax.axis_index("ctx")
    h = lax.axis_index("head")
    v = lax.axis_index("video")
    other = 1 - c
    mine = pl.multiple_of(c * tok, tok)
    theirs = pl.multiple_of(other * tok, tok)
    pairs_heads = 2 * slabs

    def columns(owner, slab):
        return pl.ds(pl.multiple_of((owner * slabs + slab) * LANE, LANE), LANE)

    loads = []
    for slab in range(slabs):
        loads.append(
            pltpu.make_async_copy(
                iqkv.at[:, 0, :, columns(c, slab)],
                i_rows.at[slab, :, pl.ds(mine, tok), :],
                load_sem.at[slab],
            )
        )
    loads.append(pltpu.make_async_copy(rate, rates.at[c], load_sem.at[2 * slabs]))
    loads.append(
        pltpu.make_async_copy(
            first_w.at[pl.ds(c * pairs_heads, pairs_heads)], fw, load_sem.at[2 * slabs + 1]
        )
    )
    loads.append(
        pltpu.make_async_copy(
            second_w.at[pl.ds(c * pairs_heads, pairs_heads)], sw, load_sem.at[2 * slabs + 2]
        )
    )
    a_loads = [
        pltpu.make_async_copy(
            aqkv.at[:, 0, :, columns(c, slab)],
            a_rows.at[slab, :, pl.ds(mine, tok), :],
            load_sem.at[slabs + slab],
        )
        for slab in range(slabs)
    ]
    ow_load = pltpu.make_async_copy(out_w, ow, load_sem.at[2 * slabs + 3])
    for copy in loads + a_loads + [ow_load]:
        copy.start()

    barrier = pltpu.get_barrier_semaphore()
    pl.semaphore_signal(
        barrier, inc=1, device_id={"ctx": other}, device_id_type=MESH_ID
    )
    below, above = v > 0, v < count - 1
    for step in range(1, count):
        pl.semaphore_signal(
            barrier,
            inc=1,
            device_id={"head": lax.rem(h + step, count)},
            device_id_type=MESH_ID,
        )

    def tell(semaphore, inside, video):
        @pl.when(inside)
        def _():
            pl.semaphore_signal(
                semaphore, inc=1, device_id={"video": video}, device_id_type=MESH_ID
            )

    tell(barrier, below, v - 1)
    tell(barrier, above, v + 1)
    pl.semaphore_wait(barrier, count + (v + count - 1) // count + (2 * count - 2 - v) // count)

    def to_partner(src, dst, send, recv):
        return pltpu.make_async_remote_copy(
            src_ref=src,
            dst_ref=dst,
            send_sem=send,
            recv_sem=recv,
            device_id={"ctx": other},
            device_id_type=MESH_ID,
        )

    rate_out = to_partner(
        rate, rates.at[c], y_send.at[2 * slabs], y_recv.at[2 * slabs]
    )
    rate_out.start()
    i_out = [
        to_partner(
            iqkv.at[:, 0, :, columns(other, slab)],
            i_rows.at[slab, :, pl.ds(mine, tok), :],
            y_send.at[slab],
            y_recv.at[slab],
        )
        for slab in range(slabs)
    ]
    a_out = [
        to_partner(
            aqkv.at[:, 0, :, columns(other, slab)],
            a_rows.at[slab, :, pl.ds(mine, tok), :],
            y_send.at[slabs + slab],
            y_recv.at[slabs + slab],
        )
        for slab in range(slabs)
    ]
    for first, second in zip(i_out, a_out):
        first.start()
        second.start()

    for semaphore, first, video, last in (
        (low_sem, below, v + 1, above),
        (high_sem, above, v - 1, below),
    ):

        @pl.when(first)
        def _(semaphore=semaphore):
            pl.semaphore_wait(semaphore, 1)

        tell(semaphore, last, video)

    seq_ids = lax.broadcasted_iota(jnp.int32, (seq, seq), 1)
    row_ids = lax.broadcasted_iota(jnp.int32, (seq, seq), 0)
    len_val = length[0]
    segs = jnp.broadcast_to(seg[...].astype(jnp.float32), (seq, seq))
    allowed = (segs == segs.T) & ((seq_ids < len_val) | (seq_ids == row_ids))
    bias[...] = jnp.where(allowed, 0.0, -1e30)
    live = (lax.broadcasted_iota(jnp.int32, (seq, LANE), 0) < len_val).astype(jnp.float32)
    left = lax.broadcasted_iota(jnp.int32, (MB, LANE), 1) < HD
    left_seq = lax.broadcasted_iota(jnp.int32, (seq, LANE), 1) < HD
    tri = lax.broadcasted_iota(jnp.int32, (MB, MB), 0) >= lax.broadcasted_iota(
        jnp.int32, (MB, MB), 1
    )
    tri = tri.astype(jnp.float32)
    tri_pair = jnp.concatenate([tri, tri], axis=0)

    gate_s[...] = jnp.tanh(gate[...].reshape(1, gate.shape[0]))

    for copy in loads:
        copy.wait()

    def pair_row(ref, head):
        return jnp.concatenate([ref[pl.ds(head, 1), :], ref[pl.ds(head + 1, 1), :]], axis=1)

    for slab in range(slabs):
        head = c * pairs_heads + 2 * slab
        gain_s[slab] = pair_row(gain, head)
        shift_s[slab] = pair_row(shift, head)
        b1[slab] = pair_row(first_b, head)
        b2[slab] = pair_row(second_b, head)
        for raw, kept, used in ((fw, w1m, w1b), (sw, w2m, w2b)):
            upper, lower = raw[2 * slab], raw[2 * slab + 1]
            kept[slab, 0:HD] = upper.astype(jnp.float32)
            kept[slab, HD:LANE] = lower.astype(jnp.float32)
            used[slab] = jnp.zeros_like(used[slab])
            used[slab, 0:HD, 0:hidden] = upper
            used[slab, HD:LANE, hidden : 2 * hidden] = lower

    rate_out.wait_recv()
    for slab in range(slabs):
        head = c * pairs_heads + 2 * slab
        for part in range(seq // tok):
            rows = slice(part * tok, (part + 1) * tok)
            for ahead, store in ((0, rate_a), (1, rate_b)):
                row = rates[part, head + ahead]
                store[slab, rows] = jnp.broadcast_to(row, (LANE, tok)).T * live[rows]

    def inner_step(slab, row):
        rows = pl.ds(row, MB)
        query, key, value = (i_rows[slab, kind, rows, :] for kind in range(3))
        query_f = query.astype(jnp.float32)
        key_f = key.astype(jnp.float32)
        value_f = value.astype(jnp.float32)
        norm_gain = gain_s[slab]
        norm_shift = shift_s[slab]
        weight_one = w1b[slab]
        weight_two = w2b[slab]
        bias_one = b1[slab]
        bias_two = b2[slab]
        pre = dot_nn(jnp.concatenate([key, query], axis=0), weight_one) + bias_one
        hidden_act, slope = gelu_pair(pre[:MB])
        hidden_b = hidden_act.astype(jnp.bfloat16)
        normed, inv_std = half_stats(dot_nt(hidden_b, weight_two) + bias_two, left)
        scaled = (norm_gain * normed + norm_shift - (value_f - key_f)) * norm_gain
        grad_two = inv_std * (
            scaled - half_mean(scaled, left) - normed * half_mean(scaled * normed, left)
        )
        e_a = rate_a[slab, rows, :]
        e_b = rate_b[slab, rows, :]
        wide = [e_a] * (hidden // LANE) + [e_b] * (hidden // LANE)
        grad_one = dot_nn(grad_two.astype(jnp.bfloat16), weight_two) * slope
        grad_one = grad_one * jnp.concatenate(wide, axis=1)
        grad_two = grad_two * jnp.where(left, e_a, e_b)
        one_b = grad_one.astype(jnp.bfloat16)
        two_b = grad_two.astype(jnp.bfloat16)

        first_kernel = (dot_nt(split_heads(query, left), key) + 1.0) * tri_pair
        first_kernel = first_kernel.astype(jnp.bfloat16)
        fix = jnp.concatenate(
            [
                dot_nn(first_kernel[:MB], one_b[:, :hidden]),
                dot_nn(first_kernel[MB:], one_b[:, hidden:]),
            ],
            axis=1,
        )
        query_act = gelu_only(pre[MB:] - fix).astype(jnp.bfloat16)
        second_kernel = jnp.concatenate(
            [
                dot_nt(query_act[:, :hidden], hidden_b[:, :hidden]),
                dot_nt(query_act[:, hidden:], hidden_b[:, hidden:]),
            ],
            axis=0,
        )
        second_kernel = ((second_kernel + 1.0) * tri_pair).astype(jnp.bfloat16)
        fix_two = dot_nn(second_kernel, two_b)
        fix_two = jnp.where(left, fix_two[:MB], fix_two[MB:])
        query_out = dot_nt(query_act, weight_two) + bias_two - fix_two
        normed_out, _ = half_stats(query_out, left)
        inner[slab, rows, :] = query_f + norm_gain * normed_out + norm_shift

        for kept, used, change in (
            (w1m, w1b, dot_tn(key, one_b)),
            (w2m, w2b, dot_tn(two_b, hidden_b)),
        ):
            upper = kept[slab, 0:HD] - change[:HD, :hidden]
            lower = kept[slab, HD:LANE] - change[HD:, hidden:]
            kept[slab, 0:HD] = upper
            kept[slab, HD:LANE] = lower
            used[slab, 0:HD, 0:hidden] = upper.astype(jnp.bfloat16)
            used[slab, HD:LANE, hidden : 2 * hidden] = lower.astype(jnp.bfloat16)
        b1[slab] = bias_one - jnp.sum(grad_one, axis=0, keepdims=True)
        b2[slab] = bias_two - jnp.sum(grad_two, axis=0, keepdims=True)

    def to_video(src, video, spot, step):
        return pltpu.make_async_remote_copy(
            src_ref=src,
            dst_ref=gathered.at[v, spot],
            send_sem=z_send.at[spot, step - 1],
            recv_sem=z_recv.at[spot, step - 1],
            device_id={"video": video},
            device_id_type=MESH_ID,
        )

    def spread(src, spot):
        copies = []
        for step in range(count - 1, 0, -1):
            copy = to_video(src, lax.rem(v + step, count), spot, step)
            copy.start()
            copies.append(copy)
        return copies

    z_out = []
    backs = []
    owns = []
    for slab in range(slabs):
        i_out[slab].wait_recv()

        def batch_step(batch, carry, slab=slab):
            inner_step(slab, pl.multiple_of(batch * MB, MB))
            return carry

        lax.fori_loop(0, seq // MB, batch_step, 0, unroll=True)
        a_loads[slab].wait()
        a_out[slab].wait_recv()
        query, key, value = (a_rows[slab, kind] for kind in range(3))
        scores = dot_nt(split_heads(query, left_seq), key) * HD ** (-0.5)
        halves = []
        for part in range(2):
            mine_scores = scores[part * seq : (part + 1) * seq] + bias[...]
            top = jnp.max(mine_scores, axis=-1, keepdims=True)
            weights = jnp.exp(mine_scores - top)
            mass = jnp.sum(weights, axis=-1, keepdims=True)
            halves.append(dot_nn(weights.astype(jnp.bfloat16), value) / mass)
        attended = jnp.where(left_seq, halves[0], halves[1])
        gate_row = gate_s[:, columns(c, slab)]
        comb[slab] = ((attended + gate_row * inner[slab]) * live).astype(jnp.bfloat16)
        spot = c * slabs + slab
        back = to_partner(
            comb.at[slab, pl.ds(theirs, tok), :],
            gathered.at[v, spot],
            back_send.at[slab],
            back_recv.at[slab],
        )
        back.start()
        backs.append(back)
        own = pltpu.make_async_copy(
            comb.at[slab, pl.ds(mine, tok), :], gathered.at[v, spot], own_sem.at[slab]
        )
        own.start()
        owns.append(own)
        z_out += spread(comb.at[slab, pl.ds(mine, tok), :], spot)
        if slab:
            backs[slab - 1].wait_recv()
            far = other * slabs + slab - 1
            z_out += spread(gathered.at[v, far], far)
    backs[slabs - 1].wait_recv()
    far = other * slabs + slabs - 1
    z_out += spread(gathered.at[v, far], far)
    for own in owns:
        own.wait()
    ow_load.wait()

    def owner_of(video):
        return lax.rem(video, 2) * (count // 2) + video // 2

    def video_of(head):
        return lax.rem(head, count // 2) * 2 + head // (count // 2)

    chunks, _, _, chunk = parts.shape
    toward = 1 - 2 * (v // (count // 2))

    def part_copy(video, at):
        head = owner_of(video)
        ahead = lax.rem(head - h + count, count)
        slot = lax.rem(ahead + count - 1, count)
        return head, pltpu.make_async_remote_copy(
            src_ref=parts.at[at, video],
            dst_ref=arrived.at[at, slot],
            send_sem=r_send.at[at, slot],
            recv_sem=r_recv.at[at, slot],
            device_id={"head": head},
            device_id_type=MESH_ID,
        )

    videos = []
    for near in range(count):
        video = lax.rem(v + toward * near + count, count)
        videos.append(video)
        if near:
            step = lax.rem(v - video + count, count)
            for spot in range(2 * slabs):
                pltpu.make_async_remote_copy(
                    src_ref=gathered.at[video, spot],
                    dst_ref=gathered.at[video, spot],
                    send_sem=z_send.at[spot, step - 1],
                    recv_sem=z_recv.at[spot, step - 1],
                    device_id={"video": video},
                    device_id_type=MESH_ID,
                ).wait_recv()
        rows_video = jnp.concatenate(
            [gathered[video, spot] for spot in range(2 * slabs)], axis=1
        )
        for at in range(chunks):
            piece = dot_nn(rows_video, ow[:, at * chunk : (at + 1) * chunk])
            parts[at, video] = piece.astype(jnp.bfloat16)
            head, copy = part_copy(video, at)

            @pl.when(head != h)
            def _(copy=copy):
                copy.start()

    to_head, to_v = v, video_of(h)
    stays = (to_head == h) & (to_v == v)
    finals = []
    for at in range(chunks):
        for step in range(1, count):
            pltpu.make_async_remote_copy(
                src_ref=arrived.at[at, step - 1],
                dst_ref=arrived.at[at, step - 1],
                send_sem=r_send.at[at, step - 1],
                recv_sem=r_recv.at[at, step - 1],
                device_id={"head": lax.rem(h + step, count)},
                device_id_type=MESH_ID,
            ).wait_recv()
        summed = parts[at, video_of(h)].astype(jnp.float32)
        for step in range(count - 1):
            summed = summed + arrived[at, step].astype(jnp.float32)
        total[at] = summed.astype(jnp.bfloat16)
        final = pltpu.make_async_remote_copy(
            src_ref=total.at[at],
            dst_ref=landed.at[at],
            send_sem=t_send.at[at],
            recv_sem=t_recv.at[at],
            device_id={"head": to_head, "video": to_v},
            device_id_type=MESH_ID,
        )

        @pl.when(stays)
        def _(at=at):
            landed[at] = total[at]

        @pl.when(jnp.logical_not(stays))
        def _(final=final):
            final.start()

        finals.append(final)

    @pl.when(jnp.logical_not(stays))
    def _():
        for final in finals:
            final.wait()

    for at in range(chunks):
        out[0, :, at * chunk : (at + 1) * chunk] = landed[at]

    for copy in [rate_out] + i_out + a_out + backs + z_out:
        copy.wait_send()
    for video in videos:
        for at in range(chunks):
            head, copy = part_copy(video, at)

            @pl.when(head != h)
            def _(copy=copy):
                copy.wait_send()


def fused_on_device(
    attention_qkv,
    inner_qkv,
    learn_rate,
    segment_id,
    video_length,
    gate_alpha,
    inner_gain,
    inner_shift,
    first_weight,
    first_bias,
    second_weight,
    second_bias,
    out_weight,
):
    tok = attention_qkv.shape[2]
    width_dev = attention_qkv.shape[3]
    count = lax.axis_size("head")
    ctx_count = lax.axis_size("ctx")
    seq = tok * ctx_count
    slabs = width_dev // LANE // ctx_count
    heads = width_dev // HD
    hidden = first_weight.shape[2]
    columns = out_weight.shape[1]
    chunk = 2 * LANE if columns % (2 * LANE) == 0 else columns
    chunks = columns // chunk
    half = jnp.bfloat16
    full = jnp.float32
    hbm = pl.BlockSpec(memory_space=pl.ANY)
    vmem = pl.BlockSpec(memory_space=pltpu.VMEM)
    smem = pl.BlockSpec(memory_space=pltpu.SMEM)
    dma = pltpu.SemaphoreType.DMA
    return pl.pallas_call(
        fused_kernel,
        out_shape=jax.ShapeDtypeStruct((1, tok, columns), half),
        in_specs=[hbm] * 6 + [vmem, smem] + [vmem] * 5,
        out_specs=vmem,
        scratch_shapes=[
            pltpu.VMEM((slabs, 3, seq, LANE), half),
            pltpu.VMEM((slabs, 3, seq, LANE), half),
            pltpu.VMEM((ctx_count, heads, 1, tok), full),
            pltpu.VMEM((2 * slabs,) + first_weight.shape[1:], half),
            pltpu.VMEM((2 * slabs,) + second_weight.shape[:0:-1], half),
            pltpu.VMEM(out_weight.shape, half),
            pltpu.VMEM((slabs, LANE, hidden), full),
            pltpu.VMEM((slabs, LANE, 2 * hidden), half),
            pltpu.VMEM((slabs, LANE, hidden), full),
            pltpu.VMEM((slabs, LANE, 2 * hidden), half),
            pltpu.VMEM((slabs, 1, 2 * hidden), full),
            pltpu.VMEM((slabs, 1, LANE), full),
            pltpu.VMEM((1, width_dev), full),
            pltpu.VMEM((slabs, 1, LANE), full),
            pltpu.VMEM((slabs, 1, LANE), full),
            pltpu.VMEM((slabs, seq, LANE), full),
            pltpu.VMEM((slabs, seq, LANE), full),
            pltpu.VMEM((seq, seq), full),
            pltpu.VMEM((slabs, seq, LANE), full),
            pltpu.VMEM((slabs, seq, LANE), half),
            pltpu.VMEM((count, 2 * slabs, tok, LANE), half),
            pltpu.VMEM((chunks, count, tok, chunk), half),
            pltpu.VMEM((chunks, count - 1, tok, chunk), half),
            pltpu.VMEM((chunks, tok, chunk), half),
            pltpu.VMEM((chunks, tok, chunk), half),
            dma((2 * slabs + 4,)),
            dma((2 * slabs + 1,)),
            dma((2 * slabs + 1,)),
            dma((slabs,)),
            dma((slabs,)),
            dma((2 * slabs, count - 1)),
            dma((2 * slabs, count - 1)),
            dma((slabs,)),
            dma((chunks, count - 1)),
            dma((chunks, count - 1)),
            dma((chunks,)),
            dma((chunks,)),
            pltpu.SemaphoreType.REGULAR,
            pltpu.SemaphoreType.REGULAR,
        ],
        compiler_params=pltpu.CompilerParams(
            collective_id=0, has_side_effects=True, vmem_limit_bytes=60 * 1024 * 1024
        ),
    )(
        attention_qkv,
        inner_qkv,
        learn_rate.transpose(1, 0, 2),
        first_weight,
        second_weight.transpose(0, 2, 1),
        out_weight,
        segment_id,
        video_length,
        gate_alpha,
        inner_gain,
        inner_shift,
        first_bias,
        second_bias,
    )


def general_on_device(
    attention_qkv,
    inner_qkv,
    learn_rate,
    segment_id,
    video_length,
    gate_alpha,
    inner_gain,
    inner_shift,
    first_weight,
    first_bias,
    second_weight,
    second_bias,
    out_weight,
):
    tok_count = attention_qkv.shape[2]
    width_dev = attention_qkv.shape[3]
    heads_dev = width_dev // HD
    ctx_index = lax.axis_index("ctx")
    ctx_count = lax.axis_size("ctx")
    positions = ctx_index * tok_count + jnp.arange(tok_count, dtype=jnp.int32)
    length_val = video_length[0]
    live_rows = (positions < length_val).astype(jnp.float32)
    kv_pair = attention_qkv[1:, 0]
    kv_wide = with_halo(kv_pair, (("ctx", 1),), tok_count)
    key_pos = (ctx_index - 1) * tok_count + jnp.arange(3 * tok_count, dtype=jnp.int32)
    seg_row = segment_id[0]
    fill_ids = jnp.full((tok_count,), -1, jnp.int32)
    seg_pad = jnp.concatenate([fill_ids, seg_row, fill_ids])
    key_seg = lax.dynamic_slice_in_dim(seg_pad, ctx_index * tok_count, 3 * tok_count, 0)
    query_seg = lax.dynamic_slice_in_dim(seg_row, ctx_index * tok_count, tok_count, 0)
    allowed = (key_seg[None, :] == query_seg[:, None]) & (
        (key_pos[None, :] < length_val) | (key_pos[None, :] == positions[:, None])
    )
    query_heads = attention_qkv[0, 0].reshape(tok_count, heads_dev, HD)
    key_heads = kv_wide[0].reshape(3 * tok_count, heads_dev, HD)
    value_heads = kv_wide[1].reshape(3 * tok_count, heads_dev, HD)
    scores = jnp.einsum(
        "qhd,khd->hqk", query_heads, key_heads, preferred_element_type=jnp.float32
    ) * HD ** (-0.5)
    scores = jnp.where(allowed[None], scores, -1e30)
    row_max = jnp.max(scores, axis=-1, keepdims=True)
    exp_scores = jnp.exp(scores - row_max)
    soft_weights = (exp_scores / jnp.sum(exp_scores, axis=-1, keepdims=True)).astype(jnp.bfloat16)
    attended = jnp.einsum(
        "hqk,khd->qhd", soft_weights, value_heads, preferred_element_type=jnp.float32
    ).reshape(tok_count, width_dev)
    init_state = (
        first_weight.astype(jnp.float32),
        first_bias,
        second_weight.astype(jnp.float32),
        second_bias,
    )
    rate_rows = learn_rate[0] * live_rows[None, :]
    heads_each = -(-heads_dev // ctx_count)
    heads_padded = heads_each * ctx_count
    rows_heads = inner_qkv[:, 0].reshape(3, tok_count, heads_dev, HD)
    rows_padded = jnp.concatenate(
        [rows_heads, jnp.zeros((3, tok_count, heads_padded - heads_dev, HD), rows_heads.dtype)],
        axis=2,
    )
    rates_padded = pad_heads(rate_rows, heads_padded, 0.0)
    whole_rows = lax.all_to_all(rows_padded, "ctx", split_axis=2, concat_axis=1, tiled=True)
    whole_rates = lax.all_to_all(rates_padded, "ctx", split_axis=0, concat_axis=1, tiled=True)
    seq_count = whole_rows.shape[1]
    full_batches = seq_count // MB
    local_qkv = (
        whole_rows.astype(jnp.float32)
        .transpose(0, 2, 1, 3)
        .reshape(3, heads_each, full_batches, MB, HD)
    )
    local_rates = whole_rates.reshape(heads_each, full_batches, MB)
    first_head = ctx_index * heads_each
    local_gain = lax.dynamic_slice_in_dim(
        pad_heads(inner_gain, heads_padded, 1.0), first_head, heads_each, 0
    )
    local_shift = lax.dynamic_slice_in_dim(
        pad_heads(inner_shift, heads_padded, 0.0), first_head, heads_each, 0
    )
    local_state = tuple(
        (
            lax.dynamic_slice_in_dim(
                pad_heads(piece_arr, heads_padded, 0.0), first_head, heads_each, 0
            )
            for piece_arr in init_state
        )
    )
    unused_final, saved_local = jax.vmap(partial(chain_scan, True))(
        local_state, local_qkv[0], local_qkv[1], local_qkv[2], local_rates, local_gain, local_shift
    )
    out_rows = saved_local.reshape(heads_each, seq_count, HD).transpose(1, 0, 2)
    back_rows = lax.all_to_all(
        out_rows.astype(jnp.bfloat16), "ctx", split_axis=0, concat_axis=1, tiled=True
    ).astype(out_rows.dtype)
    inner_flat = back_rows[:, :heads_dev].reshape(tok_count, width_dev)
    combined = ((attended + jnp.tanh(gate_alpha) * inner_flat) * live_rows[:, None]).astype(
        jnp.bfloat16
    )
    terms = jnp.dot(
        combined,
        lax.all_gather(out_weight, "video", axis=1, tiled=True),
        preferred_element_type=jnp.float32,
    )
    mixed = lax.psum_scatter(terms.astype(jnp.bfloat16), "head", scatter_dimension=1, tiled=True)
    return mixed[None]


def solution(mesh):
    placed = (
        P(None, "video", "ctx", "head"),
        P(None, "video", "ctx", "head"),
        P("video", "head", "ctx"),
        P("video", None),
        P("video"),
        P("head"),
        P("head", None),
        P("head", None),
        P("head", None, None),
        P("head", None),
        P("head", None, None),
        P("head", None),
        P("head", "video"),
    )
    shape = mesh.shape
    fused = shape["ctx"] == 2 and shape["head"] == shape["video"] and shape["head"] % 2 == 0

    def on_device(*args):
        heads_dev = args[0].shape[3] // HD
        if fused and heads_dev % (2 * shape["ctx"]) == 0 and args[0].shape[2] % 128 == 0:
            return fused_on_device(*args)
        return general_on_device(*args)

    return jax.shard_map(
        on_device, mesh=mesh, in_specs=placed, out_specs=P("video", "ctx", "head"), check_vma=False
    )
```

profile of v0, /device:TPU:1, one launch (start us, length us, event | category | flops | bytes accessed | tf_op | source)
XLA Modules:
  0.0 52.0 jit_solution(2082437222271317724)
XLA Ops:
  0.7 49.7 %shard_map.127 = bf16[1,128,768]{2,1,0:T(8,128)(2,1)} custom-call(bf16[3,1,128,768]{3,2,1,0:T(8,128)(2,1)} %aqkv.1, bf16[3,1,128,768]{3,2,1,0:T(8,128)(2,1)} %iqkv.1, f32[12,1,128]{2,1,0:T(1,128)} %bitcast.3, bf16[12,64,256]{2,1,0:T(8,128)(2,1)} %first_w.1, bf16[12,64,256]{2,1,0:T(8,128)(2,1)} %bitcast.2, bf16[768,768]{1,0:T(8,128)(2,1)} %out_w.1, ...), custom_call_target="tpu_custom_call" | custom-call | tf_op jit(solution)/shard_map/pallas_call | solution.py:659
  50.4 1.6 %copy.16 = bf16[1,128,768]{2,1,0:T(8,128)(2,1)} copy(bf16[1,128,768]{2,1,0:T(8,128)(2,1)} %shard_map.127) | data formatting | bytes 393216
where the time goes:
time: 52.2 us; the launch traced here: 52 us
  Pallas kernels  49.7 us (95%)
  local copies, waits for them, and re-layouts  1.62 us (3%)
  between operations  0.66 us (1%)
    pallas_call x1, Pallas kernels, fused_on_device(): pl.pallas_call(fused_kernel, out_shape=jax.ShapeDtypeStruct((1, tok, colu...  49.7 us
    unnamed x1, local copies, waits for them, and re-layouts  1.62 us

commit v1 on v0

--- a/solution.py
+++ b/solution.py
@@ -2,6 +2,7 @@
 
 import jax
 import jax.numpy as jnp
+import numpy as np
 from jax import lax
 from jax.experimental import pallas as pl
 from jax.experimental.pallas import tpu as pltpu
@@ -142,21 +143,27 @@
     )
 
 
+def gelu_parts(entries):
+    square = entries * entries
+    inner_arg = entries * (gelu_scale + gelu_scale * gelu_cubic * square)
+    half = 0.5 + 0.5 * jnp.tanh(inner_arg)
+    return (square, half, entries * half)
+
+
 def gelu_only(entries):
-    inner_arg = gelu_scale * (entries + gelu_cubic * entries * entries * entries)
-    return 0.5 * entries * (1.0 + jnp.tanh(inner_arg))
+    return gelu_parts(entries)[2]
+
+
+def gelu_and_slope(entries):
+    square, half, act_val = gelu_parts(entries)
+    ramp = 2.0 * gelu_scale + 6.0 * gelu_scale * gelu_cubic * square
+    return (act_val, half + act_val * (1.0 - half) * ramp)
 
 
 def half_mean(cells, left):
     first = jnp.sum(jnp.where(left, cells, 0.0), axis=-1, keepdims=True)
     second = jnp.sum(jnp.where(left, 0.0, cells), axis=-1, keepdims=True)
     return jnp.where(left, first, second) * (1.0 / HD)
-
-
-def half_stats(summed, left):
-    center = summed - half_mean(summed, left)
-    inv_std = lax.rsqrt(half_mean(center * center, left) + 1e-06)
-    return (center * inv_std, inv_std)
 
 
 def split_heads(cells, left):
@@ -187,8 +194,8 @@
     fw,
     sw,
     ow,
-    w1m,
-    w1b,
+    lefts,
+    rights,
     w2m,
     w2b,
     b1,
@@ -196,8 +203,10 @@
     gate_s,
     gain_s,
     shift_s,
-    rate_a,
-    rate_b,
+    rate_s,
+    averager,
+    pickers,
+    tri_pair,
     bias,
     inner,
     comb,
@@ -328,16 +337,20 @@
         first.start()
         second.start()
 
-    for semaphore, first, video, last in (
-        (low_sem, below, v + 1, above),
-        (high_sem, above, v - 1, below),
-    ):
-
-        @pl.when(first)
-        def _(semaphore=semaphore):
-            pl.semaphore_wait(semaphore, 1)
-
-        tell(semaphore, last, video)
+    tell(low_sem, v == 0, v + 1)
+    tell(high_sem, v == count - 1, v - 1)
+
+    def pass_on(stage):
+        for semaphore, here, video, last in (
+            (low_sem, v == stage, v + 1, above),
+            (high_sem, v == count - 1 - stage, v - 1, below),
+        ):
+
+            @pl.when(here)
+            def _(semaphore=semaphore):
+                pl.semaphore_wait(semaphore, 1)
+
+            tell(semaphore, jnp.logical_and(here, last), video)
 
     seq_ids = lax.broadcasted_iota(jnp.int32, (seq, seq), 1)
     row_ids = lax.broadcasted_iota(jnp.int32, (seq, seq), 0)
@@ -348,16 +361,22 @@
     live = (lax.broadcasted_iota(jnp.int32, (seq, LANE), 0) < len_val).astype(jnp.float32)
     left = lax.broadcasted_iota(jnp.int32, (MB, LANE), 1) < HD
     left_seq = lax.broadcasted_iota(jnp.int32, (seq, LANE), 1) < HD
-    tri = lax.broadcasted_iota(jnp.int32, (MB, MB), 0) >= lax.broadcasted_iota(
-        jnp.int32, (MB, MB), 1
-    )
-    tri = tri.astype(jnp.float32)
-    tri_pair = jnp.concatenate([tri, tri], axis=0)
+    pair_row_ids = lax.broadcasted_iota(jnp.int32, (LANE, LANE), 0)
+    pair_col_ids = lax.broadcasted_iota(jnp.int32, (LANE, LANE), 1)
+    same = (pair_row_ids < HD) == (pair_col_ids < HD)
+    tri_pair[...] = jnp.where(same & (pair_row_ids >= pair_col_ids), 1.0, 0.0)
+    averager[...] = jnp.where(same, 1.0 / HD, 0.0).astype(jnp.bfloat16)
+    pickers[...] = jnp.where(pair_row_ids == pair_col_ids, 1.0, 0.0).astype(jnp.bfloat16)
+    batches = seq // MB
+    before = seq - MB
+    lane_ids = lax.broadcasted_iota(jnp.int32, (MB, LANE), 1)
+    batch_row_ids = lax.broadcasted_iota(jnp.int32, (MB, LANE), 0)
 
     gate_s[...] = jnp.tanh(gate[...].reshape(1, gate.shape[0]))
 
     for copy in loads:
         copy.wait()
+    pass_on(1)
 
     def pair_row(ref, head):
         return jnp.concatenate([ref[pl.ds(head, 1), :], ref[pl.ds(head + 1, 1), :]], axis=1)
@@ -366,90 +385,152 @@
         head = c * pairs_heads + 2 * slab
         gain_s[slab] = pair_row(gain, head)
         shift_s[slab] = pair_row(shift, head)
-        b1[slab] = pair_row(first_b, head)
-        b2[slab] = pair_row(second_b, head)
-        for raw, kept, used in ((fw, w1m, w1b), (sw, w2m, w2b)):
-            upper, lower = raw[2 * slab], raw[2 * slab + 1]
-            kept[slab, 0:HD] = upper.astype(jnp.float32)
-            kept[slab, HD:LANE] = lower.astype(jnp.float32)
-            used[slab] = jnp.zeros_like(used[slab])
-            used[slab, 0:HD, 0:hidden] = upper
-            used[slab, HD:LANE, hidden : 2 * hidden] = lower
+        bias_two = pair_row(second_b, head)
+        b2[slab, 0] = bias_two - half_mean(bias_two, left[:1])
+        for half in range(2):
+            b1[slab, half] = first_b[pl.ds(head + half, 1), :]
+            rights[slab, half, 0:before] = jnp.zeros((before, hidden), jnp.bfloat16)
+            rights[slab, half, before:seq] = fw[2 * slab + half]
+            whole = sw[2 * slab + half].astype(jnp.float32)
+            whole = whole - jnp.mean(whole, axis=0, keepdims=True)
+            w2m[slab, half * HD : (half + 1) * HD] = whole
+            w2b[slab, 0, half * HD : (half + 1) * HD] = whole.astype(jnp.bfloat16)
 
     rate_out.wait_recv()
     for slab in range(slabs):
         head = c * pairs_heads + 2 * slab
         for part in range(seq // tok):
             rows = slice(part * tok, (part + 1) * tok)
-            for ahead, store in ((0, rate_a), (1, rate_b)):
-                row = rates[part, head + ahead]
-                store[slab, rows] = jnp.broadcast_to(row, (LANE, tok)).T * live[rows]
-
-    def inner_step(slab, row):
-        rows = pl.ds(row, MB)
-        query, key, value = (i_rows[slab, kind, rows, :] for kind in range(3))
-        query_f = query.astype(jnp.float32)
+            row_a, row_b = rates[part, head], rates[part, head + 1]
+            upright = jnp.concatenate(
+                [jnp.broadcast_to(row_a, (HD, tok)), jnp.broadcast_to(row_b, (HD, tok))], axis=0
+            )
+            rate_s[slab, rows] = -(upright.T * live[rows])
+
+    def average(cells):
+        return dot_nn(cells.astype(jnp.bfloat16), averager[...])
+
+    def parted(cells):
+        return jnp.concatenate(
+            [jnp.where(left, cells, 0.0), jnp.where(left, 0.0, cells)], axis=0
+        ).astype(jnp.bfloat16)
+
+    def joined(cells):
+        return jnp.where(left, cells[:MB], cells[MB:])
+
+    def masked_tile(cells, base, limit, causal):
+        cols = np.arange(LANE)[None, :] + base
+        reach = limit + (np.arange(MB)[:, None] if causal else -1)
+        allowed = np.broadcast_to((cols <= reach) & (cols < before), (MB, LANE))
+        kept = allowed | (cols >= before)
+        if not kept.any():
+            return jnp.zeros((MB, LANE), jnp.bfloat16)
+        col_ids = lane_ids + base
+        if allowed.all():
+            cells = cells + 1.0
+        elif allowed.any():
+            inside = col_ids <= (limit + batch_row_ids if causal else limit - 1)
+            inside = inside & (col_ids < before)
+            cells = cells + jnp.where(inside, 1.0, 0.0)
+            if not kept.all():
+                cells = jnp.where(inside | (col_ids >= before), cells, 0.0)
+        elif not kept.all():
+            cells = jnp.where(col_ids >= before, cells, 0.0)
+        return cells.astype(jnp.bfloat16)
+
+    def inner_setup(slab):
+        query, key, value = (i_rows[slab, kind] for kind in range(3))
         key_f = key.astype(jnp.float32)
-        value_f = value.astype(jnp.float32)
+        key_parts = (
+            jnp.where(left_seq, key_f, 0.0).astype(jnp.bfloat16),
+            jnp.where(left_seq, 0.0, key_f).astype(jnp.bfloat16),
+        )
+        both = jnp.concatenate([key, query], axis=0)
+        for half in range(2):
+            against = jnp.concatenate(
+                [key_parts[half][:before], pickers[half * HD : (half + 1) * HD]], axis=0
+            )
+            product = dot_nt(both, against)
+            for block in range(2 * batches):
+                rows = slice(block * MB, (block + 1) * MB)
+                for base in range(0, seq, LANE):
+                    lefts[slab, half, rows, base : base + LANE] = masked_tile(
+                        product[rows, base : base + LANE],
+                        base,
+                        (block % batches) * MB,
+                        block >= batches,
+                    )
         norm_gain = gain_s[slab]
-        norm_shift = shift_s[slab]
-        weight_one = w1b[slab]
-        weight_two = w2b[slab]
-        bias_one = b1[slab]
-        bias_two = b2[slab]
-        pre = dot_nn(jnp.concatenate([key, query], axis=0), weight_one) + bias_one
-        hidden_act, slope = gelu_pair(pre[:MB])
+        pull = norm_gain * (shift_s[slab] - (value.astype(jnp.float32) - key_f))
+        last = slice(before, seq)
+        own = dot_nt(query[last], jnp.concatenate([part[last] for part in key_parts], axis=0))
+        own = ((jnp.concatenate([own, own], axis=0) + 1.0) * tri_pair[...]).astype(jnp.bfloat16)
+        return pull, average(pull), own
+
+    def query_step(slab, batch, pre, hidden_b, pair_two):
+        rows = slice(batch * MB, (batch + 1) * MB)
+        query_act = gelu_only(pre).astype(jnp.bfloat16)
+        second_kernel = (dot_nt(query_act, hidden_b) + 1.0) * tri_pair[...]
+        query_out = dot_nt(query_act, w2b[slab, batch]) + dot_nn(
+            second_kernel.astype(jnp.bfloat16), pair_two
+        )
+        query_out = joined(query_out) + b2[slab, batch]
+        inv_std = lax.rsqrt(average(query_out * query_out) + 1e-06)
+        query = i_rows[slab, 0, rows, :].astype(jnp.float32)
+        inner[slab, rows, :] = query + gain_s[slab] * (query_out * inv_std) + shift_s[slab]
+
+    def inner_step(slab, batch, prepared, waiting):
+        pull, pull_mean, own = prepared
+        rows = slice(batch * MB, (batch + 1) * MB)
+        final = batch == batches - 1
+        blocks = [batch] + ([batches + batch - 1] if batch else []) + (
+            [batches + batch] if final else []
+        )
+        pres = []
+        for half in range(2):
+            used = jnp.concatenate(
+                [lefts[slab, half, at * MB : (at + 1) * MB] for at in blocks], axis=0
+            )
+            pres.append(dot_nn(used, rights[slab, half]) + b1[slab, half])
+
+        def picked(at):
+            return jnp.concatenate([pre[at * MB : (at + 1) * MB] for pre in pres], axis=0)
+
+        hidden_act, slope = gelu_and_slope(picked(0))
         hidden_b = hidden_act.astype(jnp.bfloat16)
-        normed, inv_std = half_stats(dot_nt(hidden_b, weight_two) + bias_two, left)
-        scaled = (norm_gain * normed + norm_shift - (value_f - key_f)) * norm_gain
-        grad_two = inv_std * (
-            scaled - half_mean(scaled, left) - normed * half_mean(scaled * normed, left)
-        )
-        e_a = rate_a[slab, rows, :]
-        e_b = rate_b[slab, rows, :]
-        wide = [e_a] * (hidden // LANE) + [e_b] * (hidden // LANE)
-        grad_one = dot_nn(grad_two.astype(jnp.bfloat16), weight_two) * slope
-        grad_one = grad_one * jnp.concatenate(wide, axis=1)
-        grad_two = grad_two * jnp.where(left, e_a, e_b)
-        one_b = grad_one.astype(jnp.bfloat16)
-        two_b = grad_two.astype(jnp.bfloat16)
-
-        first_kernel = (dot_nt(split_heads(query, left), key) + 1.0) * tri_pair
-        first_kernel = first_kernel.astype(jnp.bfloat16)
-        fix = jnp.concatenate(
-            [
-                dot_nn(first_kernel[:MB], one_b[:, :hidden]),
-                dot_nn(first_kernel[MB:], one_b[:, hidden:]),
-            ],
-            axis=1,
-        )
-        query_act = gelu_only(pre[MB:] - fix).astype(jnp.bfloat16)
-        second_kernel = jnp.concatenate(
-            [
-                dot_nt(query_act[:, :hidden], hidden_b[:, :hidden]),
-                dot_nt(query_act[:, hidden:], hidden_b[:, hidden:]),
-            ],
-            axis=0,
-        )
-        second_kernel = ((second_kernel + 1.0) * tri_pair).astype(jnp.bfloat16)
-        fix_two = dot_nn(second_kernel, two_b)
-        fix_two = jnp.where(left, fix_two[:MB], fix_two[MB:])
-        query_out = dot_nt(query_act, weight_two) + bias_two - fix_two
-        normed_out, _ = half_stats(query_out, left)
-        inner[slab, rows, :] = query_f + norm_gain * normed_out + norm_shift
-
-        for kept, used, change in (
-            (w1m, w1b, dot_tn(key, one_b)),
-            (w2m, w2b, dot_tn(two_b, hidden_b)),
-        ):
-            upper = kept[slab, 0:HD] - change[:HD, :hidden]
-            lower = kept[slab, HD:LANE] - change[HD:, hidden:]
-            kept[slab, 0:HD] = upper
-            kept[slab, HD:LANE] = lower
-            used[slab, 0:HD, 0:hidden] = upper.astype(jnp.bfloat16)
-            used[slab, HD:LANE, hidden : 2 * hidden] = lower.astype(jnp.bfloat16)
-        b1[slab] = bias_one - jnp.sum(grad_one, axis=0, keepdims=True)
-        b2[slab] = bias_two - jnp.sum(grad_two, axis=0, keepdims=True)
+        norm_gain = gain_s[slab]
+        squared_gain = norm_gain * norm_gain
+        bias_two = b2[slab, batch]
+        center = joined(dot_nt(hidden_b, w2b[slab, batch])) + bias_two
+        square = center * center
+        pulled = pull[rows]
+        means = average(
+            jnp.concatenate(
+                [square, squared_gain * center, squared_gain * square, pulled * center], axis=0
+            )
+        )
+        var, lin, quad, cross = (means[at * MB : (at + 1) * MB] for at in range(4))
+        inv_std = lax.rsqrt(var + 1e-06)
+        normed = center * inv_std
+        scaled = squared_gain * normed + pulled
+        along = inv_std * (inv_std * quad + cross)
+        grad_two = inv_std * (scaled - (inv_std * lin + pull_mean[rows]) - normed * along)
+        two = grad_two * rate_s[slab, rows]
+        pair_two = parted(two)
+        one = (dot_nn(pair_two, w2b[slab, batch]) * slope).astype(jnp.bfloat16)
+        if not final:
+            for half in range(2):
+                rights[slab, half, rows] = one[half * MB : (half + 1) * MB]
+            updated = w2m[slab] + dot_tn(pair_two, hidden_b)
+            w2m[slab] = updated
+            w2b[slab, batch + 1] = updated.astype(jnp.bfloat16)
+            b2[slab, batch + 1] = bias_two + jnp.sum(two, axis=0, keepdims=True)
+        if waiting is not None:
+            query_step(slab, batch - 1, picked(1), *waiting)
+        if final:
+            pre = picked(len(blocks) - 1) + dot_nn(own, one)
+            query_step(slab, batch, pre, hidden_b, pair_two)
+        return (hidden_b, pair_two)
 
     def to_video(src, video, spot, step):
         return pltpu.make_async_remote_copy(
@@ -474,14 +555,20 @@
     owns = []
     for slab in range(slabs):
         i_out[slab].wait_recv()
-
-        def batch_step(batch, carry, slab=slab):
-            inner_step(slab, pl.multiple_of(batch * MB, MB))
-            return carry
-
-        lax.fori_loop(0, seq // MB, batch_step, 0, unroll=True)
+        if slab == 0:
+            for stage in range(2, count - 1):
+                pass_on(stage)
+
+        prepared = inner_setup(slab)
+        waiting = None
+        for batch in range(batches // 2):
+            waiting = inner_step(slab, batch, prepared, waiting)
+        if slab == 0 and count > 2:
+            pass_on(count - 1)
         a_loads[slab].wait()
         a_out[slab].wait_recv()
+        for batch in range(batches // 2, batches):
+            waiting = inner_step(slab, batch, prepared, waiting)
         query, key, value = (a_rows[slab, kind] for kind in range(3))
         scores = dot_nt(split_heads(query, left_seq), key) * HD ** (-0.5)
         halves = []
@@ -668,17 +755,19 @@
             pltpu.VMEM((2 * slabs,) + first_weight.shape[1:], half),
             pltpu.VMEM((2 * slabs,) + second_weight.shape[:0:-1], half),
             pltpu.VMEM(out_weight.shape, half),
+            pltpu.VMEM((slabs, 2, 2 * seq, seq), half),
+            pltpu.VMEM((slabs, 2, seq, hidden), half),
             pltpu.VMEM((slabs, LANE, hidden), full),
-            pltpu.VMEM((slabs, LANE, 2 * hidden), half),
-            pltpu.VMEM((slabs, LANE, hidden), full),
-            pltpu.VMEM((slabs, LANE, 2 * hidden), half),
-            pltpu.VMEM((slabs, 1, 2 * hidden), full),
-            pltpu.VMEM((slabs, 1, LANE), full),
+            pltpu.VMEM((slabs, seq // MB, LANE, hidden), half),
+            pltpu.VMEM((slabs, 2, 1, hidden), full),
+            pltpu.VMEM((slabs, seq // MB, 1, LANE), full),
             pltpu.VMEM((1, width_dev), full),
             pltpu.VMEM((slabs, 1, LANE), full),
             pltpu.VMEM((slabs, 1, LANE), full),
             pltpu.VMEM((slabs, seq, LANE), full),
-            pltpu.VMEM((slabs, seq, LANE), full),
+            pltpu.VMEM((LANE, LANE), half),
+            pltpu.VMEM((LANE, LANE), half),
+            pltpu.VMEM((LANE, LANE), full),
             pltpu.VMEM((seq, seq), full),
             pltpu.VMEM((slabs, seq, LANE), full),
             pltpu.VMEM((slabs, seq, LANE), half),

time: 52.2 us -> 51.6 us (0.989)
  Pallas kernels: 49.7 us -> 49.1 us
    pallas_call x1, Pallas kernels: 49.7 us -> 49.1 us  [fused_on_device(): pl.pallas_call(fused_kernel, out_shape=jax.ShapeDtypeStruct((1, tok, colu...]
where the time goes in v1:
time: 51.6 us; the launch traced here: 51.4 us
  Pallas kernels  49.1 us (95%)
  local copies, waits for them, and re-layouts  1.62 us (3%)
  between operations  0.66 us (1%)
    pallas_call x1, Pallas kernels, fused_on_device(): pl.pallas_call(fused_kernel, out_shape=jax.ShapeDtypeStruct((1, tok, colu...  49.1 us
    unnamed x1, local copies, waits for them, and re-layouts  1.62 us

profile of v1, /device:TPU:1, one launch (start us, length us, event | category | flops | bytes accessed | tf_op | source)
XLA Modules:
  0.0 51.4 jit_solution(9425812572328526514)
XLA Ops:
  0.7 49.1 %shard_map.127 = bf16[1,128,768]{2,1,0:T(8,128)(2,1)} custom-call(bf16[3,1,128,768]{3,2,1,0:T(8,128)(2,1)} %aqkv.1, bf16[3,1,128,768]{3,2,1,0:T(8,128)(2,1)} %iqkv.1, f32[12,1,128]{2,1,0:T(1,128)} %bitcast.3, bf16[12,64,256]{2,1,0:T(8,128)(2,1)} %first_w.1, bf16[12,64,256]{2,1,0:T(8,128)(2,1)} %bitcast.2, bf16[768,768]{1,0:T(8,128)(2,1)} %out_w.1, ...), custom_call_target="tpu_custom_call" | custom-call | tf_op jit(solution)/shard_map/pallas_call | solution.py:746
  49.8 1.6 %copy.16 = bf16[1,128,768]{2,1,0:T(8,128)(2,1)} copy(bf16[1,128,768]{2,1,0:T(8,128)(2,1)} %shard_map.127) | data formatting | bytes 393216

commit v2 on v1

--- a/solution.py
+++ b/solution.py
@@ -211,7 +211,10 @@
     inner,
     comb,
     gathered,
+    sums,
     parts,
+    beside,
+    crossing,
     arrived,
     total,
     landed,
@@ -223,6 +226,8 @@
     z_send,
     z_recv,
     own_sem,
+    s_send,
+    s_recv,
     r_send,
     r_recv,
     t_send,
@@ -312,30 +317,31 @@
         )
 
     rate_out = to_partner(
-        rate, rates.at[c], y_send.at[2 * slabs], y_recv.at[2 * slabs]
+        rate, rates.at[c], y_send.at[6 * slabs], y_recv.at[6 * slabs]
     )
     rate_out.start()
-    i_out = [
-        to_partner(
-            iqkv.at[:, 0, :, columns(other, slab)],
-            i_rows.at[slab, :, pl.ds(mine, tok), :],
-            y_send.at[slab],
-            y_recv.at[slab],
-        )
-        for slab in range(slabs)
-    ]
-    a_out = [
-        to_partner(
-            aqkv.at[:, 0, :, columns(other, slab)],
-            a_rows.at[slab, :, pl.ds(mine, tok), :],
-            y_send.at[slabs + slab],
-            y_recv.at[slabs + slab],
-        )
-        for slab in range(slabs)
-    ]
-    for first, second in zip(i_out, a_out):
-        first.start()
-        second.start()
+
+    def rows_out(source, target, slab, base):
+        return [
+            to_partner(
+                source.at[kind, 0, :, columns(other, slab)],
+                target.at[slab, kind, pl.ds(mine, tok), :],
+                y_send.at[base + 3 * slab + kind],
+                y_recv.at[base + 3 * slab + kind],
+            )
+            for kind in range(3)
+        ]
+
+    i_out = [rows_out(iqkv, i_rows, slab, 0) for slab in range(slabs)]
+    a_out = [rows_out(aqkv, a_rows, slab, 3 * slabs) for slab in range(slabs)]
+    early = max(slabs - 1, 1)
+
+    def start_rows(part):
+        for copies in zip(i_out[part], a_out[part]):
+            for copy in copies[0] + copies[1]:
+                copy.start()
+
+    start_rows(slice(0, early))
 
     tell(low_sem, v == 0, v + 1)
     tell(high_sem, v == count - 1, v - 1)
@@ -544,7 +550,7 @@
 
     def spread(src, spot):
         copies = []
-        for step in range(count - 1, 0, -1):
+        for step in range(1, count):
             copy = to_video(src, lax.rem(v + step, count), spot, step)
             copy.start()
             copies.append(copy)
@@ -554,11 +560,11 @@
     backs = []
     owns = []
     for slab in range(slabs):
-        i_out[slab].wait_recv()
+        for copy in i_out[slab]:
+            copy.wait_recv()
         if slab == 0:
             for stage in range(2, count - 1):
                 pass_on(stage)
-
         prepared = inner_setup(slab)
         waiting = None
         for batch in range(batches // 2):
@@ -566,9 +572,8 @@
         if slab == 0 and count > 2:
             pass_on(count - 1)
         a_loads[slab].wait()
-        a_out[slab].wait_recv()
-        for batch in range(batches // 2, batches):
-            waiting = inner_step(slab, batch, prepared, waiting)
+        for copy in a_out[slab]:
+            copy.wait_recv()
         query, key, value = (a_rows[slab, kind] for kind in range(3))
         scores = dot_nt(split_heads(query, left_seq), key) * HD ** (-0.5)
         halves = []
@@ -579,6 +584,12 @@
             mass = jnp.sum(weights, axis=-1, keepdims=True)
             halves.append(dot_nn(weights.astype(jnp.bfloat16), value) / mass)
         attended = jnp.where(left_seq, halves[0], halves[1])
+        for batch in range(batches // 2, batches):
+            if slab and batch == batches // 2:
+                backs[slab - 1].wait_recv()
+                far = other * slabs + slab - 1
+                z_out += spread(gathered.at[v, far], far)
+            waiting = inner_step(slab, batch, prepared, waiting)
         gate_row = gate_s[:, columns(c, slab)]
         comb[slab] = ((attended + gate_row * inner[slab]) * live).astype(jnp.bfloat16)
         spot = c * slabs + slab
@@ -590,88 +601,140 @@
         )
         back.start()
         backs.append(back)
+        if slab == 0:
+            start_rows(slice(early, slabs))
         own = pltpu.make_async_copy(
             comb.at[slab, pl.ds(mine, tok), :], gathered.at[v, spot], own_sem.at[slab]
         )
         own.start()
         owns.append(own)
         z_out += spread(comb.at[slab, pl.ds(mine, tok), :], spot)
-        if slab:
-            backs[slab - 1].wait_recv()
-            far = other * slabs + slab - 1
-            z_out += spread(gathered.at[v, far], far)
+    ow_load.wait()
+    for own in owns[:-1]:
+        own.wait()
+
+    chunks, _, _, chunk = parts.shape
+    toward = 1 - 2 * (v // (count // 2))
+    videos = [lax.rem(v + toward * near + count, count) for near in range(count)]
+
+    def z_wait(video, spots):
+        step = lax.rem(v - video + count, count)
+        for spot in spots:
+            pltpu.make_async_remote_copy(
+                src_ref=gathered.at[video, spot],
+                dst_ref=gathered.at[video, spot],
+                send_sem=z_send.at[spot, step - 1],
+                recv_sem=z_recv.at[spot, step - 1],
+                device_id={"video": video},
+                device_id_type=MESH_ID,
+            ).wait_recv()
+
+    def rows_of(video, spots):
+        return jnp.concatenate([gathered[video, spot] for spot in spots], axis=1)
+
+    first_half = list(range(slabs - 1))
+    second_half = list(range(slabs, 2 * slabs - 1))
+    last_spots = [slabs - 1, 2 * slabs - 1]
+
+    def begin(near):
+        if slabs == 1:
+            return
+        video = videos[near]
+        if near:
+            z_wait(video, first_half + second_half)
+        sums[near] = dot_nn(
+            rows_of(video, first_half), ow[0 : (slabs - 1) * LANE]
+        ) + dot_nn(
+            rows_of(video, second_half), ow[slabs * LANE : (2 * slabs - 1) * LANE]
+        )
+
+    lane_of, core_of = h // 2, lax.rem(h, 2)
+    sibling = 2 * lane_of + 1 - core_of
+    across = 2 * (1 - lane_of) + core_of
+
+    def owner_lane(video):
+        return lax.rem(video + v, 2)
+
+    def owner_core(video):
+        return lax.rem(video // 2 + v // 2, 2)
+
+    def owned(lane, core):
+        return 2 * lax.rem(core + v // 2, 2) + lax.rem(lane + v, 2)
+
+    def to_head_copy(src, dst, send, recv, head):
+        return pltpu.make_async_remote_copy(
+            src_ref=src,
+            dst_ref=dst,
+            send_sem=send,
+            recv_sem=recv,
+            device_id={"head": head},
+            device_id_type=MESH_ID,
+        )
+
+    def part_copy(video, at):
+        slot = lax.rem(owner_lane(video) + lane_of, 2)
+        return to_head_copy(
+            parts.at[at, video],
+            beside.at[at, slot],
+            s_send.at[at, slot],
+            s_recv.at[at, slot],
+            sibling,
+        )
+
+    def finish(near):
+        video = videos[near]
+        if near:
+            z_wait(video, last_spots)
+        rows_video = rows_of(video, last_spots)
+        for at in range(chunks):
+            cols = slice(at * chunk, (at + 1) * chunk)
+            piece = dot_nn(
+                rows_video,
+                jnp.concatenate(
+                    [ow[spot * LANE : (spot + 1) * LANE, cols] for spot in last_spots], axis=0
+                ),
+            )
+            if slabs > 1:
+                piece = piece + sums[near, :, cols]
+            parts[at, video] = piece.astype(jnp.bfloat16)
+            copy = part_copy(video, at)
+
+            @pl.when(owner_core(video) != core_of)
+            def _(copy=copy):
+                copy.start()
+
+    begin(0)
     backs[slabs - 1].wait_recv()
     far = other * slabs + slabs - 1
     z_out += spread(gathered.at[v, far], far)
-    for own in owns:
-        own.wait()
-    ow_load.wait()
-
-    def owner_of(video):
-        return lax.rem(video, 2) * (count // 2) + video // 2
-
-    def video_of(head):
-        return lax.rem(head, count // 2) * 2 + head // (count // 2)
-
-    chunks, _, _, chunk = parts.shape
-    toward = 1 - 2 * (v // (count // 2))
-
-    def part_copy(video, at):
-        head = owner_of(video)
-        ahead = lax.rem(head - h + count, count)
-        slot = lax.rem(ahead + count - 1, count)
-        return head, pltpu.make_async_remote_copy(
-            src_ref=parts.at[at, video],
-            dst_ref=arrived.at[at, slot],
-            send_sem=r_send.at[at, slot],
-            recv_sem=r_recv.at[at, slot],
-            device_id={"head": head},
-            device_id_type=MESH_ID,
-        )
-
-    videos = []
-    for near in range(count):
-        video = lax.rem(v + toward * near + count, count)
-        videos.append(video)
-        if near:
-            step = lax.rem(v - video + count, count)
-            for spot in range(2 * slabs):
-                pltpu.make_async_remote_copy(
-                    src_ref=gathered.at[video, spot],
-                    dst_ref=gathered.at[video, spot],
-                    send_sem=z_send.at[spot, step - 1],
-                    recv_sem=z_recv.at[spot, step - 1],
-                    device_id={"video": video},
-                    device_id_type=MESH_ID,
-                ).wait_recv()
-        rows_video = jnp.concatenate(
-            [gathered[video, spot] for spot in range(2 * slabs)], axis=1
-        )
-        for at in range(chunks):
-            piece = dot_nn(rows_video, ow[:, at * chunk : (at + 1) * chunk])
-            parts[at, video] = piece.astype(jnp.bfloat16)
-            head, copy = part_copy(video, at)
-
-            @pl.when(head != h)
-            def _(copy=copy):
-                copy.start()
-
-    to_head, to_v = v, video_of(h)
+    owns[-1].wait()
+    finish(0)
+    for near in range(1, count):
+        begin(near)
+    for near in range(1, count):
+        finish(near)
+
+    home, away = owned(lane_of, core_of), owned(1 - lane_of, core_of)
+    x_out = []
+    for at in range(chunks):
+        part_copy(away, at).wait_recv()
+        crossing[at] = (
+            parts[at, away].astype(jnp.float32) + beside[at, 1].astype(jnp.float32)
+        ).astype(jnp.bfloat16)
+        copy = to_head_copy(
+            crossing.at[at], arrived.at[at], r_send.at[at], r_recv.at[at], across
+        )
+        copy.start()
+        x_out.append(copy)
+
+    to_head, to_v = v, home
     stays = (to_head == h) & (to_v == v)
     finals = []
     for at in range(chunks):
-        for step in range(1, count):
-            pltpu.make_async_remote_copy(
-                src_ref=arrived.at[at, step - 1],
-                dst_ref=arrived.at[at, step - 1],
-                send_sem=r_send.at[at, step - 1],
-                recv_sem=r_recv.at[at, step - 1],
-                device_id={"head": lax.rem(h + step, count)},
-                device_id_type=MESH_ID,
-            ).wait_recv()
-        summed = parts[at, video_of(h)].astype(jnp.float32)
-        for step in range(count - 1):
-            summed = summed + arrived[at, step].astype(jnp.float32)
+        part_copy(home, at).wait_recv()
+        summed = parts[at, home].astype(jnp.float32) + beside[at, 0].astype(jnp.float32)
+        x_out[at].wait_recv()
+        summed = summed + arrived[at].astype(jnp.float32)
         total[at] = summed.astype(jnp.bfloat16)
         final = pltpu.make_async_remote_copy(
             src_ref=total.at[at],
@@ -700,15 +763,12 @@
     for at in range(chunks):
         out[0, :, at * chunk : (at + 1) * chunk] = landed[at]
 
-    for copy in [rate_out] + i_out + a_out + backs + z_out:
+    rows_sent = [copy for copies in i_out + a_out for copy in copies]
+    for copy in [rate_out] + rows_sent + backs + z_out + x_out:
         copy.wait_send()
-    for video in videos:
+    for lane in range(2):
         for at in range(chunks):
-            head, copy = part_copy(video, at)
-
-            @pl.when(head != h)
-            def _(copy=copy):
-                copy.wait_send()
+            part_copy(owned(lane, 1 - core_of), at).wait_send()
 
 
 def fused_on_device(
@@ -772,20 +832,25 @@
             pltpu.VMEM((slabs, seq, LANE), full),
             pltpu.VMEM((slabs, seq, LANE), half),
             pltpu.VMEM((count, 2 * slabs, tok, LANE), half),
+            pltpu.VMEM((count, tok, columns), full),
             pltpu.VMEM((chunks, count, tok, chunk), half),
-            pltpu.VMEM((chunks, count - 1, tok, chunk), half),
+            pltpu.VMEM((chunks, 2, tok, chunk), half),
+            pltpu.VMEM((chunks, tok, chunk), half),
+            pltpu.VMEM((chunks, tok, chunk), half),
             pltpu.VMEM((chunks, tok, chunk), half),
             pltpu.VMEM((chunks, tok, chunk), half),
             dma((2 * slabs + 4,)),
-            dma((2 * slabs + 1,)),
-            dma((2 * slabs + 1,)),
+            dma((6 * slabs + 1,)),
+            dma((6 * slabs + 1,)),
             dma((slabs,)),
             dma((slabs,)),
             dma((2 * slabs, count - 1)),
             dma((2 * slabs, count - 1)),
             dma((slabs,)),
-            dma((chunks, count - 1)),
-            dma((chunks, count - 1)),
+            dma((chunks, 2)),
+            dma((chunks, 2)),
+            dma((chunks,)),
+            dma((chunks,)),
             dma((chunks,)),
             dma((chunks,)),
             pltpu.SemaphoreType.REGULAR,
@@ -935,7 +1000,7 @@
         P("head", "video"),
     )
     shape = mesh.shape
-    fused = shape["ctx"] == 2 and shape["head"] == shape["video"] and shape["head"] % 2 == 0
+    fused = shape["ctx"] == 2 and shape["head"] == shape["video"] == 4
 
     def on_device(*args):
         heads_dev = args[0].shape[3] // HD

time: 51.6 us -> 49.3 us (0.955)
  Pallas kernels: 49.1 us -> 46.8 us
    pallas_call x1, Pallas kernels: 49.1 us -> 46.8 us  [fused_on_device(): pl.pallas_call(fused_kernel, out_shape=jax.ShapeDtypeStruct((1, tok, colu...]
where the time goes in v2:
time: 49.3 us; the launch traced here: 49.1 us
  Pallas kernels  46.8 us (95%)
  local copies, waits for them, and re-layouts  1.62 us (3%)
  between operations  0.66 us (1%)
    pallas_call x1, Pallas kernels, fused_on_device(): pl.pallas_call(fused_kernel, out_shape=jax.ShapeDtypeStruct((1, tok, colu...  46.8 us
    unnamed x1, local copies, waits for them, and re-layouts  1.62 us

profile of v2, /device:TPU:1, one launch (start us, length us, event | category | flops | bytes accessed | tf_op | source)
XLA Modules:
  0.0 49.1 jit_solution(14228781301651548673)
XLA Ops:
  0.7 46.8 %shard_map.127 = bf16[1,128,768]{2,1,0:T(8,128)(2,1)} custom-call(bf16[3,1,128,768]{3,2,1,0:T(8,128)(2,1)} %aqkv.1, bf16[3,1,128,768]{3,2,1,0:T(8,128)(2,1)} %iqkv.1, f32[12,1,128]{2,1,0:T(1,128)} %bitcast.3, bf16[12,64,256]{2,1,0:T(8,128)(2,1)} %first_w.1, bf16[12,64,256]{2,1,0:T(8,128)(2,1)} %bitcast.2, bf16[768,768]{1,0:T(8,128)(2,1)} %out_w.1, ...), custom_call_target="tpu_custom_call" | custom-call | tf_op jit(solution)/shard_map/pallas_call | solution.py:806
  47.5 1.6 %copy.16 = bf16[1,128,768]{2,1,0:T(8,128)(2,1)} copy(bf16[1,128,768]{2,1,0:T(8,128)(2,1)} %shard_map.127) | data formatting | bytes 393216

commit v3 on v2

--- a/solution.py
+++ b/solution.py
@@ -180,6 +180,14 @@
     first_w,
     second_w,
     out_w,
+    seg_in,
+    length_in,
+    gate_in,
+    gain_in,
+    shift_in,
+    first_b_in,
+    second_b_in,
+    out,
     seg,
     length,
     gate,
@@ -187,7 +195,7 @@
     shift,
     first_b,
     second_b,
-    out,
+    small_sem,
     a_rows,
     i_rows,
     rates,
@@ -208,6 +216,11 @@
     pickers,
     tri_pair,
     bias,
+    pulls,
+    pull_means,
+    own_s,
+    hiddens,
+    twos,
     inner,
     comb,
     gathered,
@@ -217,7 +230,6 @@
     crossing,
     arrived,
     total,
-    landed,
     load_sem,
     y_send,
     y_recv,
@@ -225,6 +237,7 @@
     back_recv,
     z_send,
     z_recv,
+    relay_send,
     own_sem,
     s_send,
     s_recv,
@@ -250,6 +263,28 @@
     def columns(owner, slab):
         return pl.ds(pl.multiple_of((owner * slabs + slab) * LANE, LANE), LANE)
 
+    barrier = pltpu.get_barrier_semaphore()
+    pl.semaphore_signal(
+        barrier, inc=1, device_id={"ctx": other}, device_id_type=MESH_ID
+    )
+    below, above = v > 0, v < count - 1
+    for step in range(1, count):
+        pl.semaphore_signal(
+            barrier,
+            inc=1,
+            device_id={"head": lax.rem(h + step, count)},
+            device_id_type=MESH_ID,
+        )
+
+    def tell(semaphore, inside, video):
+        @pl.when(inside)
+        def _():
+            pl.semaphore_signal(
+                semaphore, inc=1, device_id={"video": video}, device_id_type=MESH_ID
+            )
+
+    tell(barrier, below, v - 1)
+    tell(barrier, above, v + 1)
     loads = []
     for slab in range(slabs):
         loads.append(
@@ -282,28 +317,22 @@
     for copy in loads + a_loads + [ow_load]:
         copy.start()
 
-    barrier = pltpu.get_barrier_semaphore()
-    pl.semaphore_signal(
-        barrier, inc=1, device_id={"ctx": other}, device_id_type=MESH_ID
-    )
-    below, above = v > 0, v < count - 1
-    for step in range(1, count):
-        pl.semaphore_signal(
-            barrier,
-            inc=1,
-            device_id={"head": lax.rem(h + step, count)},
-            device_id_type=MESH_ID,
-        )
-
-    def tell(semaphore, inside, video):
-        @pl.when(inside)
-        def _():
-            pl.semaphore_signal(
-                semaphore, inc=1, device_id={"video": video}, device_id_type=MESH_ID
+    small_loads = [
+        pltpu.make_async_copy(source, kept_in, small_sem.at[at])
+        for at, (source, kept_in) in enumerate(
+            (
+                (seg_in, seg),
+                (length_in, length),
+                (gate_in, gate),
+                (gain_in, gain),
+                (shift_in, shift),
+                (first_b_in, first_b),
+                (second_b_in, second_b),
             )
-
-    tell(barrier, below, v - 1)
-    tell(barrier, above, v + 1)
+        )
+    ]
+    for copy in small_loads:
+        copy.start()
     pl.semaphore_wait(barrier, count + (v + count - 1) // count + (2 * count - 2 - v) // count)
 
     def to_partner(src, dst, send, recv):
@@ -358,6 +387,8 @@
 
             tell(semaphore, jnp.logical_and(here, last), video)
 
+    for copy in small_loads:
+        copy.wait()
     seq_ids = lax.broadcasted_iota(jnp.int32, (seq, seq), 1)
     row_ids = lax.broadcasted_iota(jnp.int32, (seq, seq), 0)
     len_val = length[0]
@@ -382,7 +413,6 @@
 
     for copy in loads:
         copy.wait()
-    pass_on(1)
 
     def pair_row(ref, head):
         return jnp.concatenate([ref[pl.ds(head, 1), :], ref[pl.ds(head + 1, 1), :]], axis=1)
@@ -401,17 +431,6 @@
             whole = whole - jnp.mean(whole, axis=0, keepdims=True)
             w2m[slab, half * HD : (half + 1) * HD] = whole
             w2b[slab, 0, half * HD : (half + 1) * HD] = whole.astype(jnp.bfloat16)
-
-    rate_out.wait_recv()
-    for slab in range(slabs):
-        head = c * pairs_heads + 2 * slab
-        for part in range(seq // tok):
-            rows = slice(part * tok, (part + 1) * tok)
-            row_a, row_b = rates[part, head], rates[part, head + 1]
-            upright = jnp.concatenate(
-                [jnp.broadcast_to(row_a, (HD, tok)), jnp.broadcast_to(row_b, (HD, tok))], axis=0
-            )
-            rate_s[slab, rows] = -(upright.T * live[rows])
 
     def average(cells):
         return dot_nn(cells.astype(jnp.bfloat16), averager[...])
@@ -444,36 +463,56 @@
             cells = jnp.where(col_ids >= before, cells, 0.0)
         return cells.astype(jnp.bfloat16)
 
-    def inner_setup(slab):
-        query, key, value = (i_rows[slab, kind] for kind in range(3))
-        key_f = key.astype(jnp.float32)
+    def inner_setup(slab, part):
+        rows = slice(part * tok, (part + 1) * tok)
+        head = c * pairs_heads + 2 * slab
+        upright = jnp.concatenate(
+            [jnp.broadcast_to(rates[part, head + half], (HD, tok)) for half in range(2)], axis=0
+        )
+        rate_s[slab, rows] = -(upright.T * live[rows])
+        known = min((part + 1) * tok, before)
+        query, key, value = (i_rows[slab, kind, rows] for kind in range(3))
+        both = jnp.concatenate([key, query], axis=0)
+        keys = i_rows[slab, 1, 0 : (part + 1) * tok].astype(jnp.float32)
+        left_keys = left_seq[0 : (part + 1) * tok]
         key_parts = (
-            jnp.where(left_seq, key_f, 0.0).astype(jnp.bfloat16),
-            jnp.where(left_seq, 0.0, key_f).astype(jnp.bfloat16),
-        )
-        both = jnp.concatenate([key, query], axis=0)
+            jnp.where(left_keys, keys, 0.0).astype(jnp.bfloat16),
+            jnp.where(left_keys, 0.0, keys).astype(jnp.bfloat16),
+        )
+        spare = [jnp.zeros((before - known, LANE), jnp.bfloat16)] if known < before else []
+        blocks = tok // MB
         for half in range(2):
             against = jnp.concatenate(
-                [key_parts[half][:before], pickers[half * HD : (half + 1) * HD]], axis=0
+                [key_parts[half][:known]] + spare + [pickers[half * HD : (half + 1) * HD]], axis=0
             )
             product = dot_nt(both, against)
-            for block in range(2 * batches):
-                rows = slice(block * MB, (block + 1) * MB)
+            for block in range(2 * blocks):
+                batch = part * blocks + block % blocks
+                causal = block >= blocks
+                target = causal * seq + batch * MB
                 for base in range(0, seq, LANE):
-                    lefts[slab, half, rows, base : base + LANE] = masked_tile(
-                        product[rows, base : base + LANE],
+                    lefts[slab, half, target : target + MB, base : base + LANE] = masked_tile(
+                        product[block * MB : (block + 1) * MB, base : base + LANE],
                         base,
-                        (block % batches) * MB,
-                        block >= batches,
+                        batch * MB,
+                        causal,
                     )
-        norm_gain = gain_s[slab]
-        pull = norm_gain * (shift_s[slab] - (value.astype(jnp.float32) - key_f))
-        last = slice(before, seq)
-        own = dot_nt(query[last], jnp.concatenate([part[last] for part in key_parts], axis=0))
-        own = ((jnp.concatenate([own, own], axis=0) + 1.0) * tri_pair[...]).astype(jnp.bfloat16)
-        return pull, average(pull), own
-
-    def query_step(slab, batch, pre, hidden_b, pair_two):
+        key_f = key.astype(jnp.float32)
+        pull = gain_s[slab] * (shift_s[slab] - (value.astype(jnp.float32) - key_f))
+        pulls[slab, rows] = pull
+        pull_means[slab, rows] = average(pull)
+        if (part + 1) * tok == seq:
+            last = slice(before, seq)
+            own = dot_nt(
+                query[before - part * tok :],
+                jnp.concatenate([cells[last] for cells in key_parts], axis=0),
+            )
+            own = (jnp.concatenate([own, own], axis=0) + 1.0) * tri_pair[...]
+            own_s[slab] = own.astype(jnp.bfloat16)
+
+    def query_step(slab, batch, pre):
+        hidden_b = hiddens[slab, batch]
+        pair_two = twos[slab, batch]
         rows = slice(batch * MB, (batch + 1) * MB)
         query_act = gelu_only(pre).astype(jnp.bfloat16)
         second_kernel = (dot_nt(query_act, hidden_b) + 1.0) * tri_pair[...]
@@ -485,8 +524,7 @@
         query = i_rows[slab, 0, rows, :].astype(jnp.float32)
         inner[slab, rows, :] = query + gain_s[slab] * (query_out * inv_std) + shift_s[slab]
 
-    def inner_step(slab, batch, prepared, waiting):
-        pull, pull_mean, own = prepared
+    def inner_step(slab, batch):
         rows = slice(batch * MB, (batch + 1) * MB)
         final = batch == batches - 1
         blocks = [batch] + ([batches + batch - 1] if batch else []) + (
@@ -504,12 +542,13 @@
 
         hidden_act, slope = gelu_and_slope(picked(0))
         hidden_b = hidden_act.astype(jnp.bfloat16)
+        hiddens[slab, batch] = hidden_b
         norm_gain = gain_s[slab]
         squared_gain = norm_gain * norm_gain
         bias_two = b2[slab, batch]
         center = joined(dot_nt(hidden_b, w2b[slab, batch])) + bias_two
         square = center * center
-        pulled = pull[rows]
+        pulled = pulls[slab, rows]
         means = average(
             jnp.concatenate(
                 [square, squared_gain * center, squared_gain * square, pulled * center], axis=0
@@ -520,9 +559,10 @@
         normed = center * inv_std
         scaled = squared_gain * normed + pulled
         along = inv_std * (inv_std * quad + cross)
-        grad_two = inv_std * (scaled - (inv_std * lin + pull_mean[rows]) - normed * along)
+        grad_two = inv_std * (scaled - (inv_std * lin + pull_means[slab, rows]) - normed * along)
         two = grad_two * rate_s[slab, rows]
         pair_two = parted(two)
+        twos[slab, batch] = pair_two
         one = (dot_nn(pair_two, w2b[slab, batch]) * slope).astype(jnp.bfloat16)
         if not final:
             for half in range(2):
@@ -531,12 +571,10 @@
             w2m[slab] = updated
             w2b[slab, batch + 1] = updated.astype(jnp.bfloat16)
             b2[slab, batch + 1] = bias_two + jnp.sum(two, axis=0, keepdims=True)
-        if waiting is not None:
-            query_step(slab, batch - 1, picked(1), *waiting)
+        if batch:
+            query_step(slab, batch - 1, picked(1))
         if final:
-            pre = picked(len(blocks) - 1) + dot_nn(own, one)
-            query_step(slab, batch, pre, hidden_b, pair_two)
-        return (hidden_b, pair_two)
+            query_step(slab, batch, picked(len(blocks) - 1) + dot_nn(own_s[slab], one))
 
     def to_video(src, video, spot, step):
         return pltpu.make_async_remote_copy(
@@ -548,32 +586,71 @@
             device_id_type=MESH_ID,
         )
 
+    def reached(step):
+        target = lax.rem(v + step, count)
+        return jnp.abs(target - v) < count - 1
+
     def spread(src, spot):
         copies = []
-        for step in range(1, count):
+        for step in (2, 1, 3):
             copy = to_video(src, lax.rem(v + step, count), spot, step)
-            copy.start()
-            copies.append(copy)
+
+            copies.append((step, copy))
         return copies
+
+    def launch(copies):
+        for step, copy in copies:
+
+            @pl.when(reached(step))
+            def _(copy=copy):
+                copy.start()
+
+
+    def relays(spot):
+        found = []
+        for place, origin in ((1, count - 1), (count - 2, 0)):
+            end = count - 1 - origin
+            step = (end - origin) % count
+            found.append(
+                (
+                    place,
+                    origin,
+                    pltpu.make_async_remote_copy(
+                        src_ref=gathered.at[origin, spot],
+                        dst_ref=gathered.at[origin, spot],
+                        send_sem=relay_send.at[spot],
+                        recv_sem=z_recv.at[spot, step - 1],
+                        device_id={"video": end},
+                        device_id_type=MESH_ID,
+                    ),
+                )
+            )
+        return found
+
+    def z_arrival(video, spot, step):
+        return pltpu.make_async_remote_copy(
+            src_ref=gathered.at[video, spot],
+            dst_ref=gathered.at[video, spot],
+            send_sem=z_send.at[spot, step - 1],
+            recv_sem=z_recv.at[spot, step - 1],
+            device_id={"video": video},
+            device_id_type=MESH_ID,
+        )
+
+    def relay(spot):
+        for place, origin, copy in relays(spot):
+
+            @pl.when(v == place)
+            def _(copy=copy, origin=origin, place=place):
+                z_arrival(origin, spot, (place - origin) % count).wait_recv()
+                copy.start()
 
     z_out = []
     backs = []
     owns = []
-    for slab in range(slabs):
-        for copy in i_out[slab]:
-            copy.wait_recv()
-        if slab == 0:
-            for stage in range(2, count - 1):
-                pass_on(stage)
-        prepared = inner_setup(slab)
-        waiting = None
-        for batch in range(batches // 2):
-            waiting = inner_step(slab, batch, prepared, waiting)
-        if slab == 0 and count > 2:
-            pass_on(count - 1)
-        a_loads[slab].wait()
-        for copy in a_out[slab]:
-            copy.wait_recv()
+    half_batches = batches // 2
+
+    def attend(slab):
         query, key, value = (a_rows[slab, kind] for kind in range(3))
         scores = dot_nt(split_heads(query, left_seq), key) * HD ** (-0.5)
         halves = []
@@ -583,15 +660,68 @@
             weights = jnp.exp(mine_scores - top)
             mass = jnp.sum(weights, axis=-1, keepdims=True)
             halves.append(dot_nn(weights.astype(jnp.bfloat16), value) / mass)
-        attended = jnp.where(left_seq, halves[0], halves[1])
-        for batch in range(batches // 2, batches):
-            if slab and batch == batches // 2:
-                backs[slab - 1].wait_recv()
-                far = other * slabs + slab - 1
-                z_out += spread(gathered.at[v, far], far)
-            waiting = inner_step(slab, batch, prepared, waiting)
+        return jnp.where(left_seq, halves[0], halves[1])
+
+    def combine(slab, attended):
         gate_row = gate_s[:, columns(c, slab)]
         comb[slab] = ((attended + gate_row * inner[slab]) * live).astype(jnp.bfloat16)
+
+    @pl.when(c == 0)
+    def _():
+        for slab in range(slabs):
+            inner_setup(slab, 0)
+        for batch in range(half_batches):
+            for slab in range(slabs):
+                inner_step(slab, batch)
+
+    pass_on(1)
+    rate_out.wait_recv()
+    for slab in range(slabs):
+        for copy in i_out[slab]:
+            copy.wait_recv()
+
+        @pl.when(c == 1)
+        def _(slab=slab):
+            inner_setup(slab, 0)
+            for batch in range(half_batches):
+                inner_step(slab, batch)
+            inner_setup(slab, 1)
+            inner_step(slab, half_batches)
+
+        @pl.when(c == 0)
+        def _(slab=slab):
+            inner_setup(slab, 1)
+            for batch in range(half_batches, batches):
+                inner_step(slab, batch)
+
+        if slab == 0:
+            pass_on(2)
+        if slab:
+            far = other * slabs + slab - 1
+            far_out = spread(gathered.at[v, far], far)
+            z_out += far_out
+
+            def send_far(far_out=far_out, slab=slab):
+                backs[slab - 1].wait_recv()
+                launch(far_out)
+
+            pl.when(c == 1)(send_far)
+        a_loads[slab].wait()
+        for copy in a_out[slab]:
+            copy.wait_recv()
+        @pl.when(c == 1)
+        def _(slab=slab):
+            attended = attend(slab)
+            for batch in range(half_batches + 1, batches):
+                inner_step(slab, batch)
+            combine(slab, attended)
+
+        @pl.when(c == 0)
+        def _(slab=slab):
+            combine(slab, attend(slab))
+
+        if slab:
+            pl.when(c == 0)(send_far)
         spot = c * slabs + slab
         back = to_partner(
             comb.at[slab, pl.ds(theirs, tok), :],
@@ -608,7 +738,15 @@
         )
         own.start()
         owns.append(own)
-        z_out += spread(comb.at[slab, pl.ds(mine, tok), :], spot)
+        if slab == 0:
+            pass_on(3)
+        near_out = spread(comb.at[slab, pl.ds(mine, tok), :], spot)
+        launch(near_out)
+        z_out += near_out
+        if slab:
+            relay(spot - 1)
+        if slab > 1:
+            relay(other * slabs + slab - 2)
     ow_load.wait()
     for own in owns[:-1]:
         own.wait()
@@ -619,15 +757,12 @@
 
     def z_wait(video, spots):
         step = lax.rem(v - video + count, count)
-        for spot in spots:
-            pltpu.make_async_remote_copy(
-                src_ref=gathered.at[video, spot],
-                dst_ref=gathered.at[video, spot],
-                send_sem=z_send.at[spot, step - 1],
-                recv_sem=z_recv.at[spot, step - 1],
-                device_id={"video": video},
-                device_id_type=MESH_ID,
-            ).wait_recv()
+        passed = ((v == 1) & (video == count - 1)) | ((v == count - 2) & (video == 0))
+
+        @pl.when(jnp.logical_not(passed))
+        def _():
+            for spot in spots:
+                z_arrival(video, spot, step).wait_recv()
 
     def rows_of(video, spots):
         return jnp.concatenate([gathered[video, spot] for spot in spots], axis=1)
@@ -685,87 +820,122 @@
         video = videos[near]
         if near:
             z_wait(video, last_spots)
-        rows_video = rows_of(video, last_spots)
+        rest = jnp.concatenate(
+            [ow[spot * LANE : (spot + 1) * LANE] for spot in last_spots], axis=0
+        )
+        piece = dot_nn(rows_of(video, last_spots), rest)
+        if slabs > 1:
+            piece = piece + sums[near]
+        piece = piece.astype(jnp.bfloat16)
         for at in range(chunks):
-            cols = slice(at * chunk, (at + 1) * chunk)
-            piece = dot_nn(
-                rows_video,
-                jnp.concatenate(
-                    [ow[spot * LANE : (spot + 1) * LANE, cols] for spot in last_spots], axis=0
-                ),
-            )
-            if slabs > 1:
-                piece = piece + sums[near, :, cols]
-            parts[at, video] = piece.astype(jnp.bfloat16)
+            parts[at, video] = piece[:, at * chunk : (at + 1) * chunk]
             copy = part_copy(video, at)
 
             @pl.when(owner_core(video) != core_of)
             def _(copy=copy):
                 copy.start()
 
-    begin(0)
-    backs[slabs - 1].wait_recv()
-    far = other * slabs + slabs - 1
-    z_out += spread(gathered.at[v, far], far)
-    owns[-1].wait()
-    finish(0)
-    for near in range(1, count):
-        begin(near)
-    for near in range(1, count):
-        finish(near)
-
     home, away = owned(lane_of, core_of), owned(1 - lane_of, core_of)
-    x_out = []
-    for at in range(chunks):
-        part_copy(away, at).wait_recv()
-        crossing[at] = (
-            parts[at, away].astype(jnp.float32) + beside[at, 1].astype(jnp.float32)
-        ).astype(jnp.bfloat16)
-        copy = to_head_copy(
-            crossing.at[at], arrived.at[at], r_send.at[at], r_recv.at[at], across
-        )
-        copy.start()
-        x_out.append(copy)
-
     to_head, to_v = v, home
     stays = (to_head == h) & (to_v == v)
-    finals = []
-    for at in range(chunks):
-        part_copy(home, at).wait_recv()
-        summed = parts[at, home].astype(jnp.float32) + beside[at, 0].astype(jnp.float32)
-        x_out[at].wait_recv()
-        summed = summed + arrived[at].astype(jnp.float32)
-        total[at] = summed.astype(jnp.bfloat16)
-        final = pltpu.make_async_remote_copy(
+    x_out = [
+        to_head_copy(crossing.at[at], arrived.at[at], r_send.at[at], r_recv.at[at], across)
+        for at in range(chunks)
+    ]
+    finals = [
+        pltpu.make_async_remote_copy(
             src_ref=total.at[at],
-            dst_ref=landed.at[at],
+            dst_ref=out.at[0, :, at * chunk : (at + 1) * chunk],
             send_sem=t_send.at[at],
             recv_sem=t_recv.at[at],
             device_id={"head": to_head, "video": to_v},
             device_id_type=MESH_ID,
         )
-
-        @pl.when(stays)
-        def _(at=at):
-            landed[at] = total[at]
-
-        @pl.when(jnp.logical_not(stays))
-        def _(final=final):
-            final.start()
-
-        finals.append(final)
+        for at in range(chunks)
+    ]
+
+    kept = [
+        pltpu.make_async_copy(
+            total.at[at], out.at[0, :, at * chunk : (at + 1) * chunk], t_send.at[at]
+        )
+        for at in range(chunks)
+    ]
+
+    def cross(near):
+        @pl.when(videos[near] == away)
+        def _():
+            for at in range(chunks):
+                part_copy(away, at).wait_recv()
+                crossing[at] = (
+                    parts[at, away].astype(jnp.float32) + beside[at, 1].astype(jnp.float32)
+                ).astype(jnp.bfloat16)
+                x_out[at].start()
+
+    def arrive(near):
+        @pl.when(videos[near] == home)
+        def _():
+            for at in range(chunks):
+                part_copy(home, at).wait_recv()
+                x_out[at].wait_recv()
+                summed = parts[at, home].astype(jnp.float32) + beside[at, 0].astype(jnp.float32)
+                total[at] = (summed + arrived[at].astype(jnp.float32)).astype(jnp.bfloat16)
+
+                @pl.when(stays)
+                def _(at=at):
+                    kept[at].start()
+
+                @pl.when(jnp.logical_not(stays))
+                def _(at=at):
+                    finals[at].start()
+
+    begin(0)
+    backs[slabs - 1].wait_recv()
+    far = other * slabs + slabs - 1
+    far_out = spread(gathered.at[v, far], far)
+    launch(far_out)
+    z_out += far_out
+    owns[-1].wait()
+    finish(0)
+    if slabs > 1:
+        relay(far - 1)
+    relay(c * slabs + slabs - 1)
+    for near in range(1, count):
+        begin(near)
+    relay(far)
+    for near in range(1, count):
+        finish(near)
+        cross(near - 1)
+    cross(count - 1)
+    for near in range(count):
+        arrive(near)
 
     @pl.when(jnp.logical_not(stays))
     def _():
         for final in finals:
-            final.wait()
-
-    for at in range(chunks):
-        out[0, :, at * chunk : (at + 1) * chunk] = landed[at]
+            final.wait_recv()
+            final.wait_send()
+
+    @pl.when(stays)
+    def _():
+        for copy in kept:
+            copy.wait()
 
     rows_sent = [copy for copies in i_out + a_out for copy in copies]
-    for copy in [rate_out] + rows_sent + backs + z_out + x_out:
+    for copy in [rate_out] + rows_sent + backs + x_out:
         copy.wait_send()
+    for step, copy in z_out:
+
+        @pl.when(reached(step))
+        def _(copy=copy):
+            copy.wait_send()
+
+    for spot in range(2 * slabs):
+        for place, _, copy in relays(spot):
+
+            @pl.when(v == place)
+            def _(copy=copy):
+                copy.wait_send()
+
     for lane in range(2):
         for at in range(chunks):
             part_copy(owned(lane, 1 - core_of), at).wait_send()
@@ -795,20 +965,26 @@
     heads = width_dev // HD
     hidden = first_weight.shape[2]
     columns = out_weight.shape[1]
-    chunk = 2 * LANE if columns % (2 * LANE) == 0 else columns
+    chunk = LANE
     chunks = columns // chunk
     half = jnp.bfloat16
     full = jnp.float32
     hbm = pl.BlockSpec(memory_space=pl.ANY)
-    vmem = pl.BlockSpec(memory_space=pltpu.VMEM)
-    smem = pl.BlockSpec(memory_space=pltpu.SMEM)
     dma = pltpu.SemaphoreType.DMA
     return pl.pallas_call(
         fused_kernel,
         out_shape=jax.ShapeDtypeStruct((1, tok, columns), half),
-        in_specs=[hbm] * 6 + [vmem, smem] + [vmem] * 5,
-        out_specs=vmem,
+        in_specs=[hbm] * 13,
+        out_specs=hbm,
         scratch_shapes=[
+            pltpu.VMEM(segment_id.shape, segment_id.dtype),
+            pltpu.SMEM(video_length.shape, video_length.dtype),
+            pltpu.VMEM(gate_alpha.shape, full),
+            pltpu.VMEM(inner_gain.shape, full),
+            pltpu.VMEM(inner_shift.shape, full),
+            pltpu.VMEM(first_bias.shape, full),
+            pltpu.VMEM(second_bias.shape, full),
+            dma((7,)),
             pltpu.VMEM((slabs, 3, seq, LANE), half),
             pltpu.VMEM((slabs, 3, seq, LANE), half),
             pltpu.VMEM((ctx_count, heads, 1, tok), full),
@@ -830,12 +1006,16 @@
             pltpu.VMEM((LANE, LANE), full),
             pltpu.VMEM((seq, seq), full),
             pltpu.VMEM((slabs, seq, LANE), full),
+            pltpu.VMEM((slabs, seq, LANE), full),
+            pltpu.VMEM((slabs, LANE, LANE), half),
+            pltpu.VMEM((slabs, seq // MB, LANE, hidden), half),
+            pltpu.VMEM((slabs, seq // MB, LANE, LANE), half),
+            pltpu.VMEM((slabs, seq, LANE), full),
             pltpu.VMEM((slabs, seq, LANE), half),
             pltpu.VMEM((count, 2 * slabs, tok, LANE), half),
             pltpu.VMEM((count, tok, columns), full),
             pltpu.VMEM((chunks, count, tok, chunk), half),
             pltpu.VMEM((chunks, 2, tok, chunk), half),
-            pltpu.VMEM((chunks, tok, chunk), half),
             pltpu.VMEM((chunks, tok, chunk), half),
             pltpu.VMEM((chunks, tok, chunk), half),
             pltpu.VMEM((chunks, tok, chunk), half),
@@ -846,6 +1026,7 @@
             dma((slabs,)),
             dma((2 * slabs, count - 1)),
             dma((2 * slabs, count - 1)),
+            dma((2 * slabs,)),
             dma((slabs,)),
             dma((chunks, 2)),
             dma((chunks, 2)),

time: 49.3 us -> 45.5 us (0.923)
  Pallas kernels: 46.8 us -> 43.1 us
    pallas_call x1, Pallas kernels: 46.8 us -> 43.1 us  [fused_on_device(): pl.pallas_call(fused_kernel, out_shape=jax.ShapeDtypeStruct((1, tok, colu...]
where the time goes in v3:
time: 45.5 us; the launch traced here: 45.4 us
  Pallas kernels  43.1 us (95%)
  local copies, waits for them, and re-layouts  1.62 us (4%)
  between operations  0.66 us (1%)
    pallas_call x1, Pallas kernels, fused_on_device(): pl.pallas_call(fused_kernel, out_shape=jax.ShapeDtypeStruct((1, tok, colu...  43.1 us
    unnamed x1, local copies, waits for them, and re-layouts  1.62 us

profile of v3, /device:TPU:1, one launch (start us, length us, event | category | flops | bytes accessed | tf_op | source)
XLA Modules:
  0.0 45.4 jit_solution(16595902595244489847)
XLA Ops:
  0.7 43.1 %shard_map.127 = bf16[1,128,768]{2,1,0:T(8,128)(2,1)} custom-call(bf16[3,1,128,768]{3,2,1,0:T(8,128)(2,1)} %aqkv.1, bf16[3,1,128,768]{3,2,1,0:T(8,128)(2,1)} %iqkv.1, f32[12,1,128]{2,1,0:T(1,128)} %bitcast.3, bf16[12,64,256]{2,1,0:T(8,128)(2,1)} %first_w.1, bf16[12,64,256]{2,1,0:T(8,128)(2,1)} %bitcast.2, bf16[768,768]{1,0:T(8,128)(2,1)} %out_w.1, ...), custom_call_target="tpu_custom_call" | custom-call | tf_op jit(solution)/shard_map/pallas_call | solution.py:974
  43.7 1.6 %copy.16 = bf16[1,128,768]{2,1,0:T(8,128)(2,1)} copy(bf16[1,128,768]{2,1,0:T(8,128)(2,1)} %shard_map.127) | data formatting | bytes 393216

commit v4 on v3

--- a/solution.py
+++ b/solution.py
@@ -662,9 +662,21 @@
             halves.append(dot_nn(weights.astype(jnp.bfloat16), value) / mass)
         return jnp.where(left_seq, halves[0], halves[1])
 
-    def combine(slab, attended):
+    def combine(slab, attended, part):
+        rows = slice(part * tok, (part + 1) * tok)
         gate_row = gate_s[:, columns(c, slab)]
-        comb[slab] = ((attended + gate_row * inner[slab]) * live).astype(jnp.bfloat16)
+        whole = attended[rows] + gate_row * inner[slab, rows]
+        comb[slab, rows] = (whole * live[rows]).astype(jnp.bfloat16)
+
+    backs += [
+        to_partner(
+            comb.at[slab, pl.ds(theirs, tok), :],
+            gathered.at[v, c * slabs + slab],
+            back_send.at[slab],
+            back_recv.at[slab],
+        )
+        for slab in range(slabs)
+    ]
 
     @pl.when(c == 0)
     def _():
@@ -712,25 +724,22 @@
         @pl.when(c == 1)
         def _(slab=slab):
             attended = attend(slab)
+            combine(slab, attended, 0)
+            backs[slab].start()
             for batch in range(half_batches + 1, batches):
                 inner_step(slab, batch)
-            combine(slab, attended)
+            combine(slab, attended, 1)
 
         @pl.when(c == 0)
         def _(slab=slab):
-            combine(slab, attend(slab))
+            attended = attend(slab)
+            combine(slab, attended, 1)
+            backs[slab].start()
+            combine(slab, attended, 0)
 
         if slab:
             pl.when(c == 0)(send_far)
         spot = c * slabs + slab
-        back = to_partner(
-            comb.at[slab, pl.ds(theirs, tok), :],
-            gathered.at[v, spot],
-            back_send.at[slab],
-            back_recv.at[slab],
-        )
-        back.start()
-        backs.append(back)
         if slab == 0:
             start_rows(slice(early, slabs))
         own = pltpu.make_async_copy(
@@ -909,6 +918,26 @@
     for near in range(count):
         arrive(near)
 
+    rows_sent = [copy for copies in i_out + a_out for copy in copies]
+    for copy in [rate_out] + rows_sent + backs + x_out:
+        copy.wait_send()
+    for step, copy in z_out:
+
+        @pl.when(reached(step))
+        def _(copy=copy):
+            copy.wait_send()
+
+    for spot in range(2 * slabs):
+        for place, _, copy in relays(spot):
+
+            @pl.when(v == place)
+            def _(copy=copy):
+                copy.wait_send()
+
+    for lane in range(2):
+        for at in range(chunks):
+            part_copy(owned(lane, 1 - core_of), at).wait_send()
+
     @pl.when(jnp.logical_not(stays))
     def _():
         for final in finals:
@@ -919,26 +948,6 @@
     def _():
         for copy in kept:
             copy.wait()
-
-    rows_sent = [copy for copies in i_out + a_out for copy in copies]
-    for copy in [rate_out] + rows_sent + backs + x_out:
-        copy.wait_send()
-    for step, copy in z_out:
-
-        @pl.when(reached(step))
-        def _(copy=copy):
-            copy.wait_send()
-
-    for spot in range(2 * slabs):
-        for place, _, copy in relays(spot):
-
-            @pl.when(v == place)
-            def _(copy=copy):
-                copy.wait_send()
-
-    for lane in range(2):
-        for at in range(chunks):
-            part_copy(owned(lane, 1 - core_of), at).wait_send()
 
 
 def fused_on_device(
@@ -973,7 +982,7 @@
     dma = pltpu.SemaphoreType.DMA
     return pl.pallas_call(
         fused_kernel,
-        out_shape=jax.ShapeDtypeStruct((1, tok, columns), half),
+        out_shape=pltpu.VMEM((1, tok, columns), half),
         in_specs=[hbm] * 13,
         out_specs=hbm,
         scratch_shapes=[

time: 45.5 us -> 43.8 us (0.963)
  local copies, waits for them, and re-layouts: 1.62 us -> 0.68 us
  Pallas kernels: 43.1 us -> 42.4 us
    unnamed x1, local copies, waits for them, and re-layouts: 1.62 us -> 0.68 us
    pallas_call x1, Pallas kernels: 43.1 us -> 42.4 us  [fused_on_device(): pl.pallas_call(fused_kernel, out_shape=pltpu.VMEM((1, tok, columns), half...]
where the time goes in v4:
time: 43.8 us; the launch traced here: 43.7 us
  Pallas kernels  42.4 us (97%)
  local copies, waits for them, and re-layouts  0.68 us (2%)
  between operations  0.66 us (2%)
    pallas_call x1, Pallas kernels, fused_on_device(): pl.pallas_call(fused_kernel, out_shape=pltpu.VMEM((1, tok, columns), half...  42.4 us

profile of v4, /device:TPU:1, one launch (start us, length us, event | category | flops | bytes accessed | tf_op | source)
XLA Modules:
  0.0 43.7 jit_solution(3360870672970635940)
XLA Ops:
  0.7 42.4 %shard_map.127 = bf16[1,128,768]{2,1,0:T(8,128)(2,1)S(1)} custom-call(bf16[3,1,128,768]{3,2,1,0:T(8,128)(2,1)} %aqkv.1, bf16[3,1,128,768]{3,2,1,0:T(8,128)(2,1)} %iqkv.1, f32[12,1,128]{2,1,0:T(1,128)} %bitcast.3, bf16[12,64,256]{2,1,0:T(8,128)(2,1)} %first_w.1, bf16[12,64,256]{2,1,0:T(8,128)(2,1)} %bitcast.2, bf16[768,768]{1,0:T(8,128)(2,1)} %out_w.1, ...), custom_call_target="tpu_custom_call" | custom-call | tf_op jit(solution)/shard_map/pallas_call | solution.py:983
  43.0 0.7 %copy.15 = bf16[1,128,768]{2,1,0:T(8,128)(2,1)} copy(bf16[1,128,768]{2,1,0:T(8,128)(2,1)S(1)} %shard_map.127) | data formatting | bytes 393216

commit v5 on v4

--- a/solution.py
+++ b/solution.py
@@ -346,7 +346,7 @@
         )
 
     rate_out = to_partner(
-        rate, rates.at[c], y_send.at[6 * slabs], y_recv.at[6 * slabs]
+        rate, rates.at[c], y_send.at[1], y_recv.at[2 * slabs]
     )
     rate_out.start()
 
@@ -355,15 +355,23 @@
             to_partner(
                 source.at[kind, 0, :, columns(other, slab)],
                 target.at[slab, kind, pl.ds(mine, tok), :],
-                y_send.at[base + 3 * slab + kind],
-                y_recv.at[base + 3 * slab + kind],
+                y_send.at[0],
+                y_recv.at[base + slab],
             )
             for kind in range(3)
         ]
 
     i_out = [rows_out(iqkv, i_rows, slab, 0) for slab in range(slabs)]
-    a_out = [rows_out(aqkv, a_rows, slab, 3 * slabs) for slab in range(slabs)]
+    a_out = [rows_out(aqkv, a_rows, slab, slabs) for slab in range(slabs)]
     early = max(slabs - 1, 1)
+
+    def in_place(ref, send, recv):
+        return to_partner(ref, ref, send, recv)
+
+    def rows_in(target, slab, base):
+        in_place(
+            target.at[slab, :, pl.ds(theirs, tok), :], y_send.at[0], y_recv.at[base + slab]
+        ).wait_recv()
 
     def start_rows(part):
         for copies in zip(i_out[part], a_out[part]):
@@ -580,7 +588,7 @@
         return pltpu.make_async_remote_copy(
             src_ref=src,
             dst_ref=gathered.at[v, spot],
-            send_sem=z_send.at[spot, step - 1],
+            send_sem=z_send.at[0],
             recv_sem=z_recv.at[spot, step - 1],
             device_id={"video": video},
             device_id_type=MESH_ID,
@@ -618,7 +626,7 @@
                     pltpu.make_async_remote_copy(
                         src_ref=gathered.at[origin, spot],
                         dst_ref=gathered.at[origin, spot],
-                        send_sem=relay_send.at[spot],
+                        send_sem=relay_send.at[0],
                         recv_sem=z_recv.at[spot, step - 1],
                         device_id={"video": end},
                         device_id_type=MESH_ID,
@@ -631,7 +639,7 @@
         return pltpu.make_async_remote_copy(
             src_ref=gathered.at[video, spot],
             dst_ref=gathered.at[video, spot],
-            send_sem=z_send.at[spot, step - 1],
+            send_sem=z_send.at[0],
             recv_sem=z_recv.at[spot, step - 1],
             device_id={"video": video},
             device_id_type=MESH_ID,
@@ -645,7 +653,6 @@
                 z_arrival(origin, spot, (place - origin) % count).wait_recv()
                 copy.start()
 
-    z_out = []
     backs = []
     owns = []
     half_batches = batches // 2
@@ -672,7 +679,7 @@
         to_partner(
             comb.at[slab, pl.ds(theirs, tok), :],
             gathered.at[v, c * slabs + slab],
-            back_send.at[slab],
+            back_send.at[0],
             back_recv.at[slab],
         )
         for slab in range(slabs)
@@ -689,8 +696,7 @@
     pass_on(1)
     rate_out.wait_recv()
     for slab in range(slabs):
-        for copy in i_out[slab]:
-            copy.wait_recv()
+        rows_in(i_rows, slab, 0)
 
         @pl.when(c == 1)
         def _(slab=slab):
@@ -711,7 +717,6 @@
         if slab:
             far = other * slabs + slab - 1
             far_out = spread(gathered.at[v, far], far)
-            z_out += far_out
 
             def send_far(far_out=far_out, slab=slab):
                 backs[slab - 1].wait_recv()
@@ -719,8 +724,7 @@
 
             pl.when(c == 1)(send_far)
         a_loads[slab].wait()
-        for copy in a_out[slab]:
-            copy.wait_recv()
+        rows_in(a_rows, slab, slabs)
         @pl.when(c == 1)
         def _(slab=slab):
             attended = attend(slab)
@@ -751,7 +755,6 @@
             pass_on(3)
         near_out = spread(comb.at[slab, pl.ds(mine, tok), :], spot)
         launch(near_out)
-        z_out += near_out
         if slab:
             relay(spot - 1)
         if slab > 1:
@@ -820,7 +823,7 @@
         return to_head_copy(
             parts.at[at, video],
             beside.at[at, slot],
-            s_send.at[at, slot],
+            s_send.at[0],
             s_recv.at[at, slot],
             sibling,
         )
@@ -848,15 +851,15 @@
     to_head, to_v = v, home
     stays = (to_head == h) & (to_v == v)
     x_out = [
-        to_head_copy(crossing.at[at], arrived.at[at], r_send.at[at], r_recv.at[at], across)
+        to_head_copy(crossing.at[at], arrived.at[at], r_send.at[0], r_recv.at[at], across)
         for at in range(chunks)
     ]
     finals = [
         pltpu.make_async_remote_copy(
             src_ref=total.at[at],
             dst_ref=out.at[0, :, at * chunk : (at + 1) * chunk],
-            send_sem=t_send.at[at],
-            recv_sem=t_recv.at[at],
+            send_sem=t_send.at[0],
+            recv_sem=t_recv.at[0],
             device_id={"head": to_head, "video": to_v},
             device_id_type=MESH_ID,
         )
@@ -865,7 +868,7 @@
 
     kept = [
         pltpu.make_async_copy(
-            total.at[at], out.at[0, :, at * chunk : (at + 1) * chunk], t_send.at[at]
+            total.at[at], out.at[0, :, at * chunk : (at + 1) * chunk], t_send.at[0]
         )
         for at in range(chunks)
     ]
@@ -902,7 +905,6 @@
     far = other * slabs + slabs - 1
     far_out = spread(gathered.at[v, far], far)
     launch(far_out)
-    z_out += far_out
     owns[-1].wait()
     finish(0)
     if slabs > 1:
@@ -918,36 +920,29 @@
     for near in range(count):
         arrive(near)
 
-    rows_sent = [copy for copies in i_out + a_out for copy in copies]
-    for copy in [rate_out] + rows_sent + backs + x_out:
-        copy.wait_send()
-    for step, copy in z_out:
-
-        @pl.when(reached(step))
-        def _(copy=copy):
-            copy.wait_send()
-
-    for spot in range(2 * slabs):
-        for place, _, copy in relays(spot):
-
-            @pl.when(v == place)
-            def _(copy=copy):
-                copy.wait_send()
-
-    for lane in range(2):
-        for at in range(chunks):
-            part_copy(owned(lane, 1 - core_of), at).wait_send()
+    rate_out.wait_send()
+    in_place(i_rows, y_send.at[0], y_recv.at[0]).wait_send()
+    in_place(comb.at[:, 0:tok], back_send.at[0], y_recv.at[0]).wait_send()
+    in_place(parts.at[:, 0:2], s_send.at[0], y_recv.at[0]).wait_send()
+    in_place(crossing, r_send.at[0], y_recv.at[0]).wait_send()
+    at_end = (v == 0) | (v == count - 1)
+
+    @pl.when(at_end)
+    def _():
+        in_place(gathered.at[0:2], z_send.at[0], y_recv.at[0]).wait_send()
+
+    @pl.when(jnp.logical_not(at_end))
+    def _():
+        in_place(gathered.at[0:3], z_send.at[0], y_recv.at[0]).wait_send()
+        in_place(gathered.at[0], relay_send.at[0], y_recv.at[0]).wait_send()
+
+    finished = in_place(total, t_send.at[0], t_recv.at[0])
 
     @pl.when(jnp.logical_not(stays))
     def _():
-        for final in finals:
-            final.wait_recv()
-            final.wait_send()
-
-    @pl.when(stays)
-    def _():
-        for copy in kept:
-            copy.wait()
+        finished.wait_recv()
+
+    finished.wait_send()
 
 
 def fused_on_device(
@@ -1029,20 +1024,20 @@
             pltpu.VMEM((chunks, tok, chunk), half),
             pltpu.VMEM((chunks, tok, chunk), half),
             dma((2 * slabs + 4,)),
-            dma((6 * slabs + 1,)),
-            dma((6 * slabs + 1,)),
+            dma((2,)),
+            dma((2 * slabs + 1,)),
+            dma((1,)),
             dma((slabs,)),
+            dma((1,)),
+            dma((2 * slabs, count - 1)),
+            dma((1,)),
             dma((slabs,)),
-            dma((2 * slabs, count - 1)),
-            dma((2 * slabs, count - 1)),
-            dma((2 * slabs,)),
-            dma((slabs,)),
+            dma((1,)),
             dma((chunks, 2)),
-            dma((chunks, 2)),
+            dma((1,)),
             dma((chunks,)),
-            dma((chunks,)),
-            dma((chunks,)),
-            dma((chunks,)),
+            dma((1,)),
+            dma((1,)),
             pltpu.SemaphoreType.REGULAR,
             pltpu.SemaphoreType.REGULAR,
         ],

time: 43.8 us -> 43.1 us (0.984)
  Pallas kernels: 42.4 us -> 41.6 us
    pallas_call x1, Pallas kernels: 42.4 us -> 41.6 us  [fused_on_device(): pl.pallas_call(fused_kernel, out_shape=pltpu.VMEM((1, tok, columns), half...]
where the time goes in v5:
time: 43.1 us; the launch traced here: 43 us
  Pallas kernels  41.6 us (97%)
  local copies, waits for them, and re-layouts  0.68 us (2%)
  between operations  0.66 us (2%)
    pallas_call x1, Pallas kernels, fused_on_device(): pl.pallas_call(fused_kernel, out_shape=pltpu.VMEM((1, tok, columns), half...  41.6 us

profile of v5, /device:TPU:1, one launch (start us, length us, event | category | flops | bytes accessed | tf_op | source)
XLA Modules:
  0.0 43.0 jit_solution(2139778439715179920)
XLA Ops:
  0.7 41.6 %shard_map.127 = bf16[1,128,768]{2,1,0:T(8,128)(2,1)S(1)} custom-call(bf16[3,1,128,768]{3,2,1,0:T(8,128)(2,1)} %aqkv.1, bf16[3,1,128,768]{3,2,1,0:T(8,128)(2,1)} %iqkv.1, f32[12,1,128]{2,1,0:T(1,128)} %bitcast.3, bf16[12,64,256]{2,1,0:T(8,128)(2,1)} %first_w.1, bf16[12,64,256]{2,1,0:T(8,128)(2,1)} %bitcast.2, bf16[768,768]{1,0:T(8,128)(2,1)} %out_w.1, ...), custom_call_target="tpu_custom_call" | custom-call | tf_op jit(solution)/shard_map/pallas_call | solution.py:978
  42.3 0.7 %copy.15 = bf16[1,128,768]{2,1,0:T(8,128)(2,1)} copy(bf16[1,128,768]{2,1,0:T(8,128)(2,1)S(1)} %shard_map.127) | data formatting | bytes 393216

commit v6 on v5

--- a/solution.py
+++ b/solution.py
@@ -799,14 +799,17 @@
     sibling = 2 * lane_of + 1 - core_of
     across = 2 * (1 - lane_of) + core_of
 
+    swapped = lax.rem(v // 2 + v, 2)
+
     def owner_lane(video):
-        return lax.rem(video + v, 2)
+        return lax.rem(video + v + (1 - video // 2) * swapped, 2)
 
     def owner_core(video):
         return lax.rem(video // 2 + v // 2, 2)
 
     def owned(lane, core):
-        return 2 * lax.rem(core + v // 2, 2) + lax.rem(lane + v, 2)
+        upper = lax.rem(core + v // 2, 2)
+        return 2 * upper + lax.rem(lane + v + (1 - upper) * swapped, 2)
 
     def to_head_copy(src, dst, send, recv, head):
         return pltpu.make_async_remote_copy(

time: 43.1 us -> 42.6 us (0.988)
  Pallas kernels: 41.6 us -> 40.9 us
    pallas_call x1, Pallas kernels: 41.6 us -> 40.9 us  [fused_on_device(): pl.pallas_call(fused_kernel, out_shape=pltpu.VMEM((1, tok, columns), half...]
where the time goes in v6:
time: 42.6 us; the launch traced here: 42.2 us
  Pallas kernels  40.9 us (96%)
  local copies, waits for them, and re-layouts  0.68 us (2%)
  between operations  0.66 us (2%)
    pallas_call x1, Pallas kernels, fused_on_device(): pl.pallas_call(fused_kernel, out_shape=pltpu.VMEM((1, tok, columns), half...  40.9 us

profile of v6, /device:TPU:1, one launch (start us, length us, event | category | flops | bytes accessed | tf_op | source)
XLA Modules:
  0.0 42.2 jit_solution(8912233700402816318)
XLA Ops:
  0.7 40.9 %shard_map.127 = bf16[1,128,768]{2,1,0:T(8,128)(2,1)S(1)} custom-call(bf16[3,1,128,768]{3,2,1,0:T(8,128)(2,1)} %aqkv.1, bf16[3,1,128,768]{3,2,1,0:T(8,128)(2,1)} %iqkv.1, f32[12,1,128]{2,1,0:T(1,128)} %bitcast.3, bf16[12,64,256]{2,1,0:T(8,128)(2,1)} %first_w.1, bf16[12,64,256]{2,1,0:T(8,128)(2,1)} %bitcast.2, bf16[768,768]{1,0:T(8,128)(2,1)} %out_w.1, ...), custom_call_target="tpu_custom_call" | custom-call | tf_op jit(solution)/shard_map/pallas_call | solution.py:981
  41.5 0.7 %copy.15 = bf16[1,128,768]{2,1,0:T(8,128)(2,1)} copy(bf16[1,128,768]{2,1,0:T(8,128)(2,1)S(1)} %shard_map.127) | data formatting | bytes 393216

commit v7 on v6

--- a/solution.py
+++ b/solution.py
@@ -697,6 +697,8 @@
     rate_out.wait_recv()
     for slab in range(slabs):
         rows_in(i_rows, slab, 0)
+        if slab == 0:
+            pass_on(2)
 
         @pl.when(c == 1)
         def _(slab=slab):
@@ -712,8 +714,6 @@
             for batch in range(half_batches, batches):
                 inner_step(slab, batch)
 
-        if slab == 0:
-            pass_on(2)
         if slab:
             far = other * slabs + slab - 1
             far_out = spread(gathered.at[v, far], far)

time: 42.6 us -> 42.6 us (level)
  no operation moved by 1% of the time
where the time goes in v7:
time: 42.6 us; the launch traced here: 42.2 us
  Pallas kernels  40.9 us (96%)
  local copies, waits for them, and re-layouts  0.68 us (2%)
  between operations  0.66 us (2%)
    pallas_call x1, Pallas kernels, fused_on_device(): pl.pallas_call(fused_kernel, out_shape=pltpu.VMEM((1, tok, columns), half...  40.9 us

profile of v7, /device:TPU:1, one launch (start us, length us, event | category | flops | bytes accessed | tf_op | source)
XLA Modules:
  0.0 42.2 jit_solution(6272647765313227381)
XLA Ops:
  0.7 40.9 %shard_map.127 = bf16[1,128,768]{2,1,0:T(8,128)(2,1)S(1)} custom-call(bf16[3,1,128,768]{3,2,1,0:T(8,128)(2,1)} %aqkv.1, bf16[3,1,128,768]{3,2,1,0:T(8,128)(2,1)} %iqkv.1, f32[12,1,128]{2,1,0:T(1,128)} %bitcast.3, bf16[12,64,256]{2,1,0:T(8,128)(2,1)} %first_w.1, bf16[12,64,256]{2,1,0:T(8,128)(2,1)} %bitcast.2, bf16[768,768]{1,0:T(8,128)(2,1)} %out_w.1, ...), custom_call_target="tpu_custom_call" | custom-call | tf_op jit(solution)/shard_map/pallas_call | solution.py:981
  41.5 0.7 %copy.15 = bf16[1,128,768]{2,1,0:T(8,128)(2,1)} copy(bf16[1,128,768]{2,1,0:T(8,128)(2,1)S(1)} %shard_map.127) | data formatting | bytes 393216
